TPU v7x, 128 devices: a whole 4x4x4 slice. The times are simulated.
128 devices in a mesh: cfg: 2 (over core), lat: 4 (over x), seq: 16 (over z, y).
Axes of the slice: x: 4, y: 4, z: 4, core: 2. Of those that a mesh axis runs over, the one named last changes fastest.
Arguments:
- latents: float32 [24, 1024, 16], P('lat', 'seq'), may hold values from -6 to 6
- timesteps: int32 [24], P('lat'), may hold values from 0 to 999
- labels: int32 [24], P('lat'), may hold values from 0 to 999
- guidance: float32 [1], replicated, may hold values from 1.5 to 4
- keep_coef: float32 [24], P('lat'), may hold values from 0.8 to 1.2
- noise_coef: float32 [24], P('lat'), may hold values from -0.6 to -0.2
- w_patch: bfloat16 [16, 1152], replicated, may hold values from -1.5 to 1.5
- label_table: bfloat16 [1001, 1152], replicated, may hold values from -6 to 6
- w_time1: bfloat16 [256, 1152], P(None, 'lat'), may hold values from -0.375 to 0.375
- w_time2: bfloat16 [1152, 1152], P(None, 'lat'), may hold values from -0.1875 to 0.1875
- ada_weight: bfloat16 [1152, 9216], P(None, 'seq'), may hold values from -0.1875 to 0.1875
- w_qkv: bfloat16 [1152, 3456], P(None, 'seq'), may hold values from -2.9168155 to 2.9168155
- w_proj: bfloat16 [1152, 1152], P(None, 'seq'), may hold values from -0.1875 to 0.1875
- w_fc1: bfloat16 [1152, 4608], P(None, 'seq'), may hold values from -0.1875 to 0.1875
- w_fc2: bfloat16 [4608, 1152], P('seq'), may hold values from -0.09375 to 0.09375
- w_out: bfloat16 [1152, 16], replicated, may hold values from -0.1875 to 0.1875
Outputs:
- next_latents: float32 [24, 1024, 16], P('lat', 'seq', 'cfg')
All inputs are finite; a program needn't handle non-finite values.
Results may differ from a plain program's by a relative error of at most 0.009.
Values may be sent and summed in bfloat16 or wider, within the bound.
A program may use at most 192 MiB of HBM per device.

v0:
```python
import math

import jax
import jax.numpy as jnp
from jax import lax
from jax.sharding import PartitionSpec as P

D = 1152
HEADS = 16
HEAD_DIM = 72
CLASSES = 1000
FREQ = 256
GRID = 32


def swapped(value, axis, stride):
    mask = 2**stride
    pairs = [(source, source ^ mask) for source in range(lax.axis_size(axis))]
    return lax.ppermute(value, axis, pairs)


def layer_norm(values):
    average = jnp.mean(values, axis=-1, keepdims=True)
    centered = values - average
    spread = jnp.mean(centered * centered, axis=-1, keepdims=True)
    return centered * lax.rsqrt(spread + 1e-06)


def modulate(values, shifted, scaled):
    return layer_norm(values) * (1.0 + scaled[:, None, :]) + shifted[:, None, :]


def time_waves(timesteps):
    half_count = FREQ // 2
    frequency = jnp.exp(-math.log(10000.0) * jnp.arange(half_count, dtype=jnp.float32) / half_count)
    angles = timesteps.astype(jnp.float32)[:, None] * frequency[None, :]
    return jnp.concatenate([jnp.cos(angles), jnp.sin(angles)], axis=-1)


def grid_waves(positions):
    quarter = D // 4
    frequency = jnp.exp(-math.log(10000.0) * jnp.arange(quarter, dtype=jnp.float32) / quarter)
    column = (positions % GRID).astype(jnp.float32)[:, None] * frequency[None, :]
    row_angle = (positions // GRID).astype(jnp.float32)[:, None] * frequency[None, :]
    return jnp.concatenate(
        [jnp.sin(column), jnp.cos(column), jnp.sin(row_angle), jnp.cos(row_angle)], axis=-1
    )


def condition(timesteps, classes, label_table, w_time1, w_time2):
    waves = time_waves(timesteps).astype(jnp.bfloat16)
    hidden_time = jax.nn.silu(jnp.dot(waves, w_time1, preferred_element_type=jnp.float32)).astype(
        jnp.bfloat16
    )
    time_vector = jnp.dot(hidden_time, w_time2, preferred_element_type=jnp.float32)
    onehot = (classes[:, None] == jnp.arange(CLASSES + 1, dtype=jnp.int32)[None, :]).astype(
        jnp.bfloat16
    )
    return time_vector + jnp.dot(onehot, label_table, preferred_element_type=jnp.float32)


def shards(
    latents,
    timesteps,
    labels,
    guidance,
    keep_coef,
    noise_coef,
    w_patch,
    label_table,
    w_time1,
    w_time2,
    ada_weight,
    w_qkv,
    w_proj,
    w_fc1,
    w_fc2,
    w_out,
):
    lat_count, tok_count, channels = latents.shape
    model_width = w_patch.shape[1]
    side_index = lax.axis_index("cfg")
    classes = jnp.where(side_index == 0, labels, CLASSES)
    time_first, time_second = (
        lax.all_gather(w_time1, "lat", axis=1, tiled=True),
        lax.all_gather(w_time2, "lat", axis=1, tiled=True),
    )
    conditioning = condition(timesteps, classes, label_table, time_first, time_second)
    own_columns = jnp.dot(
        jax.nn.silu(conditioning).astype(jnp.bfloat16),
        ada_weight,
        preferred_element_type=jnp.float32,
    )
    modulation = lax.all_gather(own_columns, "seq", axis=1, tiled=True)
    pieces = [
        modulation[:, number * model_width : (number + 1) * model_width] for number in range(8)
    ]
    positions = lax.axis_index("seq") * tok_count + jnp.arange(tok_count, dtype=jnp.int32)
    state = jnp.dot(
        latents.reshape(-1, channels).astype(jnp.bfloat16),
        w_patch,
        preferred_element_type=jnp.float32,
    )
    state = state.reshape(lat_count, tok_count, model_width) + grid_waves(positions)[None]
    qkv_full, proj_full = (
        lax.all_gather(w_qkv, "seq", axis=1, tiled=True),
        lax.all_gather(w_proj, "seq", axis=1, tiled=True),
    )
    normed = modulate(state, pieces[0], pieces[1]).astype(jnp.bfloat16).reshape(-1, model_width)
    triple = jnp.dot(normed, qkv_full, preferred_element_type=jnp.float32).astype(jnp.bfloat16)
    queries = triple[:, :model_width].reshape(lat_count, tok_count, HEADS, HEAD_DIM)
    keys_own = triple[:, model_width : 2 * model_width].reshape(lat_count, tok_count, model_width)
    values_own = triple[:, 2 * model_width :].reshape(lat_count, tok_count, model_width)
    factor = 1.0 / math.sqrt(HEAD_DIM)
    row_best = jnp.full((lat_count, HEADS, tok_count), -1e30, jnp.float32)
    keys_part = lax.all_gather(keys_own, "seq", axis=1, tiled=True)
    values_part = lax.all_gather(values_own, "seq", axis=1, tiled=True)
    key_count = keys_part.shape[1]
    keys_heads = keys_part.reshape(lat_count, key_count, HEADS, HEAD_DIM)
    values_heads = values_part.reshape(lat_count, key_count, HEADS, HEAD_DIM)
    scores = (
        jnp.einsum("lqhd,lkhd->lhqk", queries, keys_heads, preferred_element_type=jnp.float32)
        * factor
    )
    raised = jnp.maximum(row_best, jnp.max(scores, axis=-1))
    exponent = jnp.exp(scores - raised[..., None])
    row_sums = jnp.sum(exponent, axis=-1)
    weighted = jnp.einsum(
        "lhqk,lkhd->lhqd",
        exponent.astype(jnp.bfloat16),
        values_heads,
        preferred_element_type=jnp.float32,
    )
    row_best, row_sums, weighted = (raised, row_sums, weighted)
    attended = (
        (weighted / row_sums[..., None])
        .transpose(0, 2, 1, 3)
        .reshape(-1, model_width)
        .astype(jnp.bfloat16)
    )
    projected = jnp.dot(attended, proj_full, preferred_element_type=jnp.float32)
    state = state + pieces[2][:, None, :] * projected.reshape(lat_count, tok_count, model_width)
    normed = modulate(state, pieces[3], pieces[4]).astype(jnp.bfloat16).reshape(-1, model_width)
    fc1_full, fc2_full = (
        lax.all_gather(w_fc1, "seq", axis=1, tiled=True),
        lax.all_gather(w_fc2, "seq", axis=0, tiled=True),
    )
    hidden = jax.nn.gelu(
        jnp.dot(normed, fc1_full, preferred_element_type=jnp.float32), approximate=True
    ).astype(jnp.bfloat16)
    mlp_out = jnp.dot(hidden, fc2_full, preferred_element_type=jnp.float32)
    state = state + pieces[5][:, None, :] * mlp_out.reshape(lat_count, tok_count, model_width)
    final = modulate(state, pieces[6], pieces[7]).astype(jnp.bfloat16).reshape(-1, model_width)
    noise_own = jnp.dot(final, w_out, preferred_element_type=jnp.float32).reshape(
        lat_count, tok_count, channels
    )
    half_width = channels // 2
    own_latent = lax.dynamic_slice_in_dim(latents, side_index * half_width, half_width, 2)
    partner = swapped(noise_own, "cfg", 0)
    cond_noise = jnp.where(side_index == 0, noise_own, partner)
    free_noise = jnp.where(side_index == 0, partner, noise_own)
    combined = free_noise + guidance[0] * (cond_noise - free_noise)
    guided = lax.dynamic_slice_in_dim(combined, side_index * half_width, half_width, 2)
    return keep_coef[:, None, None] * own_latent + noise_coef[:, None, None] * guided


def solution(mesh):
    return jax.shard_map(
        shards,
        mesh=mesh,
        in_specs=(
            P("lat", "seq", None),
            P("lat"),
            P("lat"),
            P(),
            P("lat"),
            P("lat"),
            P(),
            P(),
            P(None, "lat"),
            P(None, "lat"),
            P(None, "seq"),
            P(None, "seq"),
            P(None, "seq"),
            P(None, "seq"),
            P("seq", None),
            P(),
        ),
        out_specs=P("lat", "seq", "cfg"),
        check_vma=False,
    )
```

profile of v0, /device:TPU:1, one launch (start us, length us, event | category | flops | bytes accessed | tf_op | source)
XLA Modules:
  0.0 571.2 jit_solution(164010904563712114)
XLA Ops:
  6.5 0.7 all-gather.9.cloned.1.call-update
  7.3 0.7 all-gather.11.cloned.1.call-update
  8.1 0.7 convert_element_type.57
  8.7 0.8 multiply_cosine_fusion
  9.7 1.3 fusion.61
  11.0 1.2 copy-done.2
  12.6 12.5 %all_gather.27 = bf16[256,1152]{0,1:T(8,128)(2,1)S(1)} all-gather(bf16[256,288]{0,1:T(8,128)(2,1)S(1)} %copy-done.5), channel_id=1, replica_groups=mesh['cfg'=2,'lat'=4,'seq'=16] {'lat'}, dimensions={1}, use_global_device_ids=true | all-gather | bytes 737280 | tf_op jit(solution)/shard_map/all_gather | solution.py:85
  25.2 23.4 %all-gather.9.cloned.1.call-done = bf16[1152,1152]{0,1:T(8,128)(2,1)} async-done(((bf16[1152,288]{0,1:T(8,128)(2,1)}), bf16[1152,1152]{0,1:T(8,128)(2,1)}) %all-gather.9.cloned.1.call-update) | async-done | bytes 2654224 | tf_op jit(solution)/shard_map/all_gather | solution.py:86
  48.6 2.7 fusion.31
  51.3 2.1 convolution_bitcast_fusion
  53.5 21.0 %all-gather = f32[16,576,6]{1,2,0:T(8,128)S(1)} all-gather(f32[1,576,6]{1,2,0:T(8,128)S(1)} %convolution_bitcast_fusion), channel_id=1, replica_groups=mesh['cfg'=2,'lat'=4,'seq'=16] {'seq'}, dimensions={0}, use_global_device_ids=true | all-gather | bytes 235008 | tf_op jit(solution)/shard_map/all_gather | solution.py:94
  75.1 45.3 %all-gather.11.cloned.1.call-done = bf16[1152,3456]{0,1:T(8,128)(2,1)} async-done(((bf16[1152,216]{0,1:T(8,128)(2,1)}), bf16[1152,3456]{0,1:T(8,128)(2,1)}) %all-gather.11.cloned.1.call-update) | async-done | bytes 7962640 | tf_op jit(solution)/shard_map/all_gather | solution.py:106
  120.4 8.3 %convolution_convert_fusion = bf16[384,3456]{1,0:T(8,128)(2,1)S(1)} fusion(bf16[384,1152]{1,0:T(8,128)(2,1)S(1)} %bitcast.55, bf16[1152,3456]{0,1:T(8,128)(2,1)} %all-gather.11.cloned.1.call-done), kind=kOutput, calls=%fused_computation.16 | convolution fusion | flops 3058974720 | bytes 11501568 | tf_op jit(solution)/shard_map/dot_general | solution.py:110
  128.7 1.5 fusion.60
  132.6 3.6 reshape.137
  136.3 91.6 %all-gather.13.cloned.1.call-done = bf16[6,1024,1152]{2,1,0:T(8,128)(2,1)} async-done(((bf16[6,64,1152]{2,1,0:T(8,128)(2,1)}), bf16[6,1024,1152]{2,1,0:T(8,128)(2,1)}) %all-gather.13.cloned.1.call-update) | async-done | bytes 14155792 | tf_op jit(solution)/shard_map/all_gather | solution.py:116
  227.9 18.7 %copy.27 = bf16[6,1024,1152]{1,2,0:T(8,128)(2,1)} copy(bf16[6,1024,1152]{2,1,0:T(8,128)(2,1)} %all-gather.13.cloned.1.call-done) | data formatting | bytes 28311552 | tf_op jit(solution)/shard_map/all_gather | solution.py:116
  246.7 80.9 %all-gather.15.cloned.1.call-done = bf16[6,1024,1152]{2,1,0:T(8,128)(2,1)} async-done(((bf16[6,64,1152]{2,1,0:T(8,128)(2,1)}), bf16[6,1024,1152]{2,1,0:T(8,128)(2,1)}) %all-gather.15.cloned.1.call-update) | async-done | bytes 14155792 | tf_op jit(solution)/shard_map/all_gather | solution.py:117
  327.6 18.7 %copy.29 = bf16[6,1024,1152]{1,2,0:T(8,128)(2,1)} copy(bf16[6,1024,1152]{2,1,0:T(8,128)(2,1)} %all-gather.15.cloned.1.call-done) | data formatting | bytes 28311552 | tf_op jit(solution)/shard_map/all_gather | solution.py:117
  346.3 18.5 %multiply_reduce_fusion = (f32[6,16,64]{2,1,0:T(8,128)S(1)}, f32[6,16,64,1024]{3,2,1,0:T(8,128)}) fusion(bf16[6,1024,16,72]{1,3,2,0:T(8,128)(2,1)} %bitcast.48, bf16[6,64,16,72]{3,2,1,0:T(8,128)(2,1)} %reshape.137), kind=kOutput, calls=%fused_computation.1 | convolution fusion | flops 918546432 | bytes 40230912 | tf_op jit(solution)/shard_map/lqhd,lkhd->lhqk/dot_general | solution.py:122
  364.8 11.2 %fusion = f32[6,16,64]{2,1,0:T(8,128)S(1)} fusion(f32[6,16,64,1024]{3,2,1,0:T(8,128)} %get-tuple-element.29, f32[6,16,64]{2,1,0:T(8,128)S(1)} %broadcast_maximum_fusion), kind=kLoop, calls=%fused_computation.2 | loop fusion | flops 18868224 | bytes 25214976 | tf_op jit(solution)/shard_map/reduce_sum | solution.py:127
  376.0 14.7 %fusion.20 = bf16[6,64,16,72]{3,1,2,0:T(8,128)(2,1)S(1)} fusion(bf16[6,1024,16,72]{1,3,2,0:T(8,128)(2,1)} %bitcast.49, f32[6,16,64,1024]{3,2,1,0:T(8,128)} %get-tuple-element.29, f32[6,16,64]{2,1,0:T(8,128)S(1)} %broadcast_maximum_fusion, f32[6,64,16]{1,2,0:T(8,128)S(1)} %bitcast.56), kind=kOutput, calls=%fused_computation.25 | convolution fusion | flops 925728768 | bytes 40255488 | tf_op jit(solution)/shard_map/lhqk,lkhd->lhqd/dot_general | solution.py:128
  390.8 2.2 copy.30
  393.0 3.2 convert_element_type.64
  396.2 3.3 fusion.62
  400.0 0.9 copy-done.4
  401.3 56.8 %all-gather.19.cloned.1.call-done = bf16[1152,4608]{0,1:T(8,128)(2,1)} async-done(((bf16[1152,288]{0,1:T(8,128)(2,1)}), bf16[1152,4608]{0,1:T(8,128)(2,1)}) %all-gather.19.cloned.1.call-update) | async-done | bytes 10616848 | tf_op jit(solution)/shard_map/all_gather | solution.py:145
  458.1 82.9 %all-gather.21.cloned.1.call-done = bf16[4608,1152]{1,0:T(8,128)(2,1)} async-done(((bf16[288,1152]{1,0:T(8,128)(2,1)}), bf16[4608,1152]{1,0:T(8,128)(2,1)}) %all-gather.21.cloned.1.call-update) | async-done | bytes 10616848 | tf_op jit(solution)/shard_map/all_gather | solution.py:146
  540.9 17.6 %fusion.14 = f32[384,1152]{1,0:T(8,128)} fusion(bf16[4608,1152]{1,0:T(8,128)(2,1)} %all-gather.21.cloned.1.call-done, bf16[384,1152]{1,0:T(8,128)(2,1)S(1)} %bitcast.54, bf16[1152,4608]{0,1:T(8,128)(2,1)} %all-gather.19.cloned.1.call-done), kind=kOutput, calls=%fused_computation.17 | convolution fusion | flops 8169652224 | bytes 23887872 | tf_op jit(solution)/shard_map/dot_general | solution.py:151
  558.6 2.5 fusion.59
  562.0 0.7 collective-permute-start
  563.6 0.7 multiply_add_fusion.1
  (56 shorter events, 5.8 us)
Async XLA Ops:
  6.5 44.8 %copy-start = (bf16[1001,1152]{1,0:T(8,128)(2,1)S(1)}, bf16[1001,1152]{1,0:T(8,128)(2,1)}, u32[]{:S(2)}) copy-start(bf16[1001,1152]{1,0:T(8,128)(2,1)} %param.23) | copy-start | bytes 6918916
  6.5 3.2 copy-start.6
  6.5 42.0 %all-gather.9.cloned.1.call-start = ((), (), s32[]{:S(2)}) async-start(), calls=%async_computation | async-start | bytes 3317760 | tf_op jit(solution)/shard_map/all_gather | solution.py:86
  7.3 113.1 %all-gather.11.cloned.1.call-start = ((), (), s32[]{:S(2)}) async-start(), calls=%async_computation.1 | async-start | bytes 8460288 | tf_op jit(solution)/shard_map/all_gather | solution.py:106
  8.0 219.9 %all-gather.13.cloned.1.call-start = ((), (), s32[]{:S(2)}) async-start(), calls=%async_computation.2 | async-start | bytes 15040512 | tf_op jit(solution)/shard_map/all_gather | solution.py:116
  9.5 3.0 copy-start.5
  9.7 15.3 %copy-start.10 = (s32[6]{0:T(128)S(1)}, s32[6]{0:T(128)}, u32[]{:S(2)}) copy-start(s32[6]{0:T(128)} %param.18) | copy-start | bytes 76
  11.0 1.2 copy-start.2
  53.5 21.2 %copy-start.3 = (f32[6,64,1152]{2,1,0:T(8,128)S(1)}, f32[6,64,1152]{2,1,0:T(8,128)}, u32[]{:S(2)}) copy-start(f32[6,64,1152]{2,1,0:T(8,128)} %copy-done.2) | copy-start | bytes 5308420
  130.2 197.4 %all-gather.15.cloned.1.call-start = ((), (), s32[]{:S(2)}) async-start(), calls=%async_computation.3 | async-start | bytes 15040512 | tf_op jit(solution)/shard_map/all_gather | solution.py:117
  130.7 265.5 %all-gather.17.cloned.1.call-start = ((), (), s32[]{:S(2)}) async-start(), calls=%async_computation.4 | async-start | bytes 2820096 | tf_op jit(solution)/shard_map/all_gather | solution.py:107
  131.3 326.7 %all-gather.19.cloned.1.call-start = ((), (), s32[]{:S(2)}) async-start(), calls=%async_computation.5 | async-start | bytes 11280384 | tf_op jit(solution)/shard_map/all_gather | solution.py:145
  131.9 409.0 %all-gather.21.cloned.1.call-start = ((), (), s32[]{:S(2)}) async-start(), calls=%async_computation.6 | async-start | bytes 11280384 | tf_op jit(solution)/shard_map/all_gather | solution.py:146
  399.6 1.3 copy-start.4
  558.6 2.9 copy-start.9
  558.6 5.7 %copy-start.1 = (bf16[1001,1152]{1,0:T(8,128)(2,1)S(1)}, bf16[1001,1152]{1,0:T(8,128)(2,1)}, u32[]{:S(2)}) copy-start(bf16[1001,1152]{1,0:T(8,128)(2,1)} %param.23) | copy-start | bytes 6918916
  561.1 2.5 copy-start.7
  561.1 2.5 copy-start.8
  562.0 1.6 collective-permute-start
Sparse Core Ops, SparseCore 0:
  9.0 39.5 all-gather.8
  50.7 69.6 all-gather.10
  130.3 97.5 all-gather.12
  229.9 97.6 all-gather.14
  329.6 45.8 all-gather.16
  377.4 80.5 all-gather.18
  460.2 80.6 all-gather.20
where the time goes:
time: 573 us; the launch traced here: 571 us
  waiting for transfers between devices  385 us (67%)
  matrix products  69.3 us (12%)
  local copies, waits for them, and re-layouts  50.5 us (9%)
  blocking collectives  33.4 us (6%)
  other arithmetic  17.8 us (3%)
  between operations  14.4 us (3%)
    all_gather x1, waiting for transfers between devices, shards(): keys_part = lax.all_gather(keys_own, 'seq', axis=1, tiled=True)  91.6 us
    all_gather x1, waiting for transfers between devices, shards(): lax.all_gather(w_fc2, 'seq', axis=0, tiled=True)  82.9 us
    all_gather x1, waiting for transfers between devices, shards(): values_part = lax.all_gather(values_own, 'seq', axis=1, tiled=True)  80.9 us
    all_gather x1, waiting for transfers between devices, shards(): lax.all_gather(w_fc1, 'seq', axis=1, tiled=True)  56.8 us
    all_gather x1, waiting for transfers between devices, shards(): lax.all_gather(w_qkv, 'seq', axis=1, tiled=True)  45.3 us
    all_gather x1, waiting for transfers between devices, shards(): lax.all_gather(w_time2, 'lat', axis=1, tiled=True)  23.4 us
    all_gather x1, blocking collectives, shards(): modulation = lax.all_gather(own_columns, 'seq', axis=1, tiled=True)  21 us
    all_gather x1, local copies, waits for them, and re-layouts, shards(): keys_part = lax.all_gather(keys_own, 'seq', axis=1, tiled=True)  18.7 us
  transfers between devices with their start and end apart: 8, of which 7 were waited for; matrix products, arithmetic and copies ran while one was open for 18% of the time, Pallas kernels for 0%

commit v1 on v0

v1 whole, which is shorter than its diff:
```python
import math

import jax
import jax.numpy as jnp
import numpy as np
from jax import lax
from jax.experimental import pallas as pl
from jax.experimental.pallas import tpu as pltpu
from jax.sharding import PartitionSpec as P

D = 1152
HEADS = 16
HEAD_DIM = 72
CLASSES = 1000
FREQ = 256
GRID = 32
TOKENS = 1024
BASE = 16 + 2 * GRID
ROWS = 96
LANES = 128
Q_ROWS = 256
F32 = jnp.float32
BF16 = jnp.bfloat16
NT = (((1,), (1,)), ((), ()))
NN = (((1,), (0,)), ((), ()))
HIGH = lax.Precision.HIGHEST


def position_rows():
    quarter = D // 4
    frequency = np.exp(-math.log(10000.0) * np.arange(quarter) / quarter)
    angle = np.arange(GRID)[:, None] * frequency[None, :]
    waves = np.concatenate([np.sin(angle), np.cos(angle)], axis=1)
    rows = np.zeros((2 * GRID, D))
    rows[:GRID, : D // 2] = waves
    rows[GRID:, D // 2 :] = waves
    return rows


def dot(a, b, dims=NN, precision=None):
    return lax.dot_general(a, b, dims, precision=precision, preferred_element_type=F32)


def layer_norm(values):
    average = jnp.mean(values, axis=-1, keepdims=True)
    centered = values - average
    spread = jnp.mean(centered * centered, axis=-1, keepdims=True)
    return centered * lax.rsqrt(spread + 1e-06)


def time_waves(timesteps):
    half_count = FREQ // 2
    frequency = jnp.exp(-math.log(10000.0) * jnp.arange(half_count, dtype=F32) / half_count)
    angles = timesteps.astype(F32)[:, None] * frequency[None, :]
    return jnp.concatenate([jnp.cos(angles), jnp.sin(angles)], axis=-1)


def attend_kernel(
    lat_ref, patch_ref, pos_ref, shift_ref, scale_ref, wq_ref, wk_ref, wv_ref,
    out_ref, ft_ref, base_ref, xs_ref, tq_ref, tv_ref, tk_ref, rstd_ref, rcol_ref, q_ref, v_ref, kt_ref,
):
    count = lat_ref.shape[0]
    patch = patch_ref[...].astype(F32)
    base_ref[:16, :] = patch - jnp.mean(patch, axis=1, keepdims=True)
    base_ref[16:, :] = pos_ref[...]
    base = base_ref[...]
    gram = dot(base, base, NT, HIGH) * (1.0 / D)
    token = lax.broadcasted_iota(jnp.int32, (2 * GRID, TOKENS), 1)
    place = lax.broadcasted_iota(jnp.int32, (2 * GRID, TOKENS), 0)
    hot = jnp.where(jnp.where(place < GRID, token % GRID, token // GRID + GRID) == place, 1.0, 0.0).astype(BF16)
    rstd_ref[...] = jnp.zeros_like(rstd_ref)
    for l in range(count):
        ft_ref[l, :16, :] = lat_ref[l]
        ft_ref[l, 16:, :] = hot
        ft = ft_ref[l].astype(F32)
        spread = jnp.sum(dot(gram, ft, NN, HIGH) * ft, axis=0, keepdims=True)
        rstd_ref[l : l + 1, :] = lax.rsqrt(spread + 1e-06)
        xs_ref[l * ROWS : l * ROWS + BASE, :] = (base * (1.0 + scale_ref[l : l + 1, :])).astype(BF16)
        xs_ref[l * ROWS + BASE : (l + 1) * ROWS, :] = jnp.broadcast_to(
            shift_ref[l : l + 1, :], (ROWS - BASE, D)
        ).astype(BF16)
    rcol_ref[...] = jnp.transpose(rstd_ref[...])
    factor = math.log2(math.e) / math.sqrt(HEAD_DIM)
    tq_ref[...] = dot(xs_ref[...], wq_ref[...], NT) * factor
    tv_ref[...] = dot(xs_ref[...], wv_ref[...], NT)
    for l in range(count):
        tk_ref[l] = dot(wk_ref[...], xs_ref[l * ROWS : (l + 1) * ROWS, :], NT)
    ones_lane = lax.broadcasted_iota(jnp.int32, (TOKENS, LANES), 1) == HEAD_DIM
    v_ref[...] = jnp.where(ones_lane, 1.0, 0.0).astype(BF16)

    def one_latent(l, carry):
        ft = ft_ref[l]
        f = jnp.transpose(ft.astype(F32)).astype(BF16)
        lane = lax.broadcasted_iota(jnp.int32, (TOKENS, LANES), 1)
        column = jnp.sum(jnp.where(lane == l, rcol_ref[...], 0.0), axis=1, keepdims=True)
        top = pl.multiple_of(l * ROWS, ROWS)
        tq = tq_ref[pl.ds(top, ROWS), :]
        tv = tv_ref[pl.ds(top, ROWS), :]
        tk = tk_ref[l]
        q_ref[...] = (dot(f, tq[:BASE].astype(BF16)) * column + tq[BASE : BASE + 1]).astype(BF16)
        v_ref[:, :HEAD_DIM] = (dot(f, tv[:BASE].astype(BF16)) * column + tv[BASE : BASE + 1]).astype(BF16)
        kt_ref[...] = (
            dot(tk[:, :BASE].astype(BF16), ft) * rstd_ref[pl.ds(l, 1), :] + tk[:, BASE : BASE + 1]
        ).astype(BF16)
        def one_block(j, carry):
            rows = pl.ds(pl.multiple_of(j * Q_ROWS, Q_ROWS), Q_ROWS)
            scores = dot(q_ref[rows, :], kt_ref[...])
            weights = jnp.exp2(scores - jnp.max(scores, axis=1, keepdims=True)).astype(BF16)
            mixed = dot(weights, v_ref[...])
            out_ref[l, rows, :] = (mixed / mixed[:, HEAD_DIM : HEAD_DIM + 1]).astype(BF16)
            return carry
        return lax.fori_loop(0, TOKENS // Q_ROWS, one_block, carry)

    lax.fori_loop(0, count, one_latent, 0)


def attend(lat, patch, shift, scale, wq, wk, wv):
    count = lat.shape[0]
    pos = position_rows()
    centred = jnp.asarray((pos - pos.mean(axis=1, keepdims=True)).astype(np.float32))
    vmem = pl.BlockSpec(memory_space=pltpu.VMEM)
    return pl.pallas_call(
        attend_kernel,
        out_shape=jax.ShapeDtypeStruct((count, TOKENS, LANES), BF16),
        in_specs=[vmem] * 8,
        out_specs=vmem,
        scratch_shapes=[
            pltpu.VMEM((count, BASE, TOKENS), BF16),
            pltpu.VMEM((BASE, D), F32),
            pltpu.VMEM((count * ROWS, D), BF16),
            pltpu.VMEM((count * ROWS, HEAD_DIM), F32),
            pltpu.VMEM((count * ROWS, HEAD_DIM), F32),
            pltpu.VMEM((count, HEAD_DIM, ROWS), F32),
            pltpu.VMEM((LANES, TOKENS), F32),
            pltpu.VMEM((TOKENS, LANES), F32),
            pltpu.VMEM((TOKENS, HEAD_DIM), BF16),
            pltpu.VMEM((TOKENS, LANES), BF16),
            pltpu.VMEM((HEAD_DIM, TOKENS), BF16),
        ],
        cost_estimate=pl.CostEstimate(flops=8 * 10**9, bytes_accessed=4 * 10**6, transcendentals=6 * 10**6),
    )(lat, patch, centred, shift, scale, wq, wk, wv)


def shards(
    latents, timesteps, labels, guidance, keep_coef, noise_coef, w_patch, label_table,
    w_time1, w_time2, ada_weight, w_qkv, w_proj, w_fc1, w_fc2, w_out,
):
    count, tok_count, channels = latents.shape
    side = lax.axis_index("cfg")
    place = lax.axis_index("seq")
    half = w_fc2.shape[0] // 2
    fc1_half = lax.dynamic_slice_in_dim(w_fc1.T, side * half, half, 0)
    fc2_half = lax.dynamic_slice_in_dim(w_fc2, side * half, half, 0)
    proj_full = lax.all_gather(w_proj.T, "seq", axis=0, tiled=True)
    fc1_full = lax.all_gather(lax.all_gather(fc1_half, "seq", axis=0, tiled=True), "cfg", axis=0, tiled=True)
    fc2_full = lax.all_gather(lax.all_gather(fc2_half, "seq", axis=0, tiled=True), "cfg", axis=0, tiled=True)

    classes = jnp.where(side == 0, labels, CLASSES)
    steps_all = lax.all_gather(timesteps, "lat", axis=0, tiled=True)
    waves = time_waves(steps_all).astype(BF16)
    hidden_own = jax.nn.silu(dot(waves, w_time1)).astype(BF16)
    hidden_time = lax.all_gather(hidden_own, "lat", axis=1, tiled=True)
    vector_own = dot(hidden_time, w_time2)
    vector = lax.all_to_all(vector_own, "lat", split_axis=0, concat_axis=1, tiled=True)
    onehot = (classes[:, None] == jnp.arange(CLASSES + 1, dtype=jnp.int32)[None, :]).astype(BF16)
    conditioning = vector + dot(onehot, label_table)
    own_columns = dot(jax.nn.silu(conditioning).astype(BF16), ada_weight)
    modulation = lax.all_gather(own_columns, "seq", axis=1, tiled=True)
    pieces = [modulation[:, number * D : (number + 1) * D] for number in range(8)]

    lat_t = jnp.transpose(latents, (0, 2, 1)).astype(BF16)
    lat_all = lax.all_gather(lat_t, "seq", axis=2, tiled=True)
    blocks = w_qkv.T.reshape(3, HEAD_DIM, D)
    got = jnp.stack(
        [
            lax.ppermute(blocks[j], "seq", [(s, (3 * s + j) % HEADS) for s in range(HEADS)])
            for j in range(3)
        ]
    )
    head_w = [lax.dynamic_index_in_dim(got, (HEADS * kind + place) % 3, 0, False) for kind in range(3)]
    attended = attend(lat_all, w_patch, pieces[0], pieces[1], *head_w)
    arrived = lax.all_to_all(
        attended[:, :, :HEAD_DIM].reshape(count, HEADS, tok_count, HEAD_DIM), "seq", split_axis=1, concat_axis=1
    )
    attended = jnp.transpose(arrived, (0, 2, 1, 3)).reshape(count * tok_count, D)

    pos = jnp.asarray(position_rows().astype(np.float32))
    columns = pos[:GRID]
    lines = lax.dynamic_slice_in_dim(pos, GRID + place * (tok_count // GRID), tok_count // GRID, 0)
    own_pos = (columns[None] + lines[:, None]).reshape(tok_count, D)
    state = dot(latents.reshape(-1, channels).astype(BF16), w_patch).reshape(count, tok_count, D) + own_pos[None]
    projected = dot(attended, proj_full, NT).reshape(count, tok_count, D)
    state = state + pieces[2][:, None, :] * projected
    normed = (layer_norm(state) * (1.0 + pieces[4][:, None, :]) + pieces[3][:, None, :]).astype(BF16).reshape(-1, D)
    hidden = jax.nn.gelu(dot(normed, fc1_full, NT), approximate=True).astype(BF16)
    mlp_out = dot(hidden, fc2_full).reshape(count, tok_count, D)
    state = state + pieces[5][:, None, :] * mlp_out
    final = (layer_norm(state) * (1.0 + pieces[7][:, None, :]) + pieces[6][:, None, :]).astype(BF16).reshape(-1, D)
    noise_own = dot(final, w_out).reshape(count, tok_count, channels)
    half_width = channels // 2
    own_latent = lax.dynamic_slice_in_dim(latents, side * half_width, half_width, 2)
    partner = lax.ppermute(noise_own, "cfg", [(0, 1), (1, 0)])
    cond_noise = jnp.where(side == 0, noise_own, partner)
    free_noise = jnp.where(side == 0, partner, noise_own)
    combined = free_noise + guidance[0] * (cond_noise - free_noise)
    guided = lax.dynamic_slice_in_dim(combined, side * half_width, half_width, 2)
    return keep_coef[:, None, None] * own_latent + noise_coef[:, None, None] * guided


def solution(mesh):
    return jax.shard_map(
        shards,
        mesh=mesh,
        in_specs=(
            P("lat", "seq", None), P("lat"), P("lat"), P(), P("lat"), P("lat"), P(), P(),
            P(None, "lat"), P(None, "lat"), P(None, "seq"), P(None, "seq"), P(None, "seq"),
            P(None, "seq"), P("seq", None), P(),
        ),
        out_specs=P("lat", "seq", "cfg"),
        check_vma=False,
    )
```

time: 573 us -> 322 us (0.56)
  waiting for transfers between devices: 385 us -> 133 us
  matrix products: 69.3 us -> 26.1 us
  starting transfers between devices: 1.13 us -> 32.7 us
  local copies, waits for them, and re-layouts: 50.5 us -> 23.1 us
  blocking collectives: 33.4 us -> 60.2 us
  Pallas kernels: 0 us -> 24.6 us
  other arithmetic: 17.8 us -> 6.03 us
    all_gather x7 -> x5, waiting for transfers between devices: 381 us -> 117 us  [the longest x1 58.5 us: shards(): lax.all_gather(fc1_half, 'seq', axis=0, tiled=True)]
    dot_general x9 -> x7, matrix products: 69.3 us -> 26.1 us  [dot(): lax.dot_general(a, b, dims, precision=precision, preferred_element_type=F32)]
    all_gather x2, local copies, waits for them, and re-layouts: 37.4 us -> 3.12 us  [the longest x1 3.09 us: shards(): lat_all = lax.all_gather(lat_t, 'seq', axis=2, tiled=True)]
    pallas_call x0 -> x1, Pallas kernels: none -> 24.6 us  [attend(): pl.pallas_call(attend_kernel, out_shape=jax.ShapeDtypeStruct((count, TOKE...]
    all_gather x1 -> x2, blocking collectives: 12.5 us -> 36.4 us  [the longest x1 27 us: shards(): lat_all = lax.all_gather(lat_t, 'seq', axis=2, tiled=True)]
    ppermute x1 -> x4, starting transfers between devices: 0.71 us -> 24.2 us  [the longest x1 15.9 us: shards(): partner = lax.ppermute(noise_own, 'cfg', [(0, 1), (1, 0)])]
    all_to_all x0 -> x2, waiting for transfers between devices: none -> 15.4 us  [the longest x1 15.4 us: shards(): lax.all_to_all(attended[:, :, :HEAD_DIM].reshape(count, HEADS, tok_count,...]
    reduce_sum x1 -> x0, other arithmetic: 11.2 us -> none  [shards(): row_sums = jnp.sum(exponent, axis=-1)]
  transfers between devices with their start and end apart: 8 -> 11, of which waited for: 7 -> 4; matrix products, arithmetic and copies ran while one was open for 18% -> 9% of each run, Pallas kernels for 0% -> 8%
where the time goes in v1:
time: 322 us; the launch traced here: 321 us
  waiting for transfers between devices  133 us (41%)
  blocking collectives  60.2 us (19%)
  starting transfers between devices  32.7 us (10%)
  matrix products  26.1 us (8%)
  Pallas kernels  24.6 us (8%)
  local copies, waits for them, and re-layouts  23.1 us (7%)
  between operations  14.8 us (5%)
  other arithmetic  6.03 us (2%)
    all_gather x1, waiting for transfers between devices, shards(): lax.all_gather(fc1_half, 'seq', axis=0, tiled=True)  58.5 us
    all_gather x1, waiting for transfers between devices, shards(): lax.all_gather(fc2_half, 'seq', axis=0, tiled=True)  58.5 us
    all_gather x1, blocking collectives, shards(): lat_all = lax.all_gather(lat_t, 'seq', axis=2, tiled=True)  27 us
    dot_general x7, matrix products, dot(): lax.dot_general(a, b, dims, precision=precision, preferred_element_type=F32)  26.1 us
    pallas_call x1, Pallas kernels, attend(): pl.pallas_call(attend_kernel, out_shape=jax.ShapeDtypeStruct((count, TOKE...  24.6 us
    all_gather x1, blocking collectives, shards(): modulation = lax.all_gather(own_columns, 'seq', axis=1, tiled=True)  16.3 us
    ppermute x1, starting transfers between devices, shards(): partner = lax.ppermute(noise_own, 'cfg', [(0, 1), (1, 0)])  15.9 us
    all_to_all x1, waiting for transfers between devices, shards(): lax.all_to_all(attended[:, :, :HEAD_DIM].reshape(count, HEADS, tok_count,...  15.4 us
  transfers between devices with their start and end apart: 11, of which 4 were waited for; matrix products, arithmetic and copies ran while one was open for 9% of the time, Pallas kernels for 8%

profile of v1, /device:TPU:1, one launch (start us, length us, event | category | flops | bytes accessed | tf_op | source)
XLA Modules:
  0.0 321.0 jit_solution(4608124997711467025)
XLA Ops:
  6.5 1.9 dynamic-slice_bitcast_fusion
  8.5 1.8 constant_dynamic-slice_fusion
  11.0 58.5 %all-gather.10.cloned.1.call-done = bf16[2304,1152]{1,0:T(8,128)(2,1)} async-done(((bf16[144,1152]{1,0:T(8,128)(2,1)}), bf16[2304,1152]{1,0:T(8,128)(2,1)}) %all-gather.10.cloned.1.call-update) | async-done | bytes 5308432 | tf_op jit(solution)/shard_map/all_gather | solution.py:155
  69.6 58.5 %all-gather.14.cloned.1.call-done = bf16[2304,1152]{1,0:T(8,128)(2,1)} async-done(((bf16[144,1152]{1,0:T(8,128)(2,1)}), bf16[2304,1152]{1,0:T(8,128)(2,1)}) %all-gather.14.cloned.1.call-update) | async-done | bytes 5308432 | tf_op jit(solution)/shard_map/all_gather | solution.py:156
  128.1 1.0 copy-done.3
  129.1 0.8 fusion.39
  129.9 1.6 collective-permute-start
  131.5 3.4 %collective-permute-start.1 = (bf16[72,1152]{1,0:T(8,128)(2,1)}, bf16[72,1152]{1,0:T(8,128)(2,1)S(1)}, u32[]{:S(2)}, u32[]{:S(2)}) collective-permute-start(bf16[72,1152]{1,0:T(8,128)(2,1)} %get-tuple-element.12), channel_id=1, source_target_pairs={{0,1},{1,4},{2,7},{3,10},{4,13},{5,0},{6,3},{7,6},{8,9},{9,12},{10... | collective-permute-start | bytes 497672 | tf_op jit(solution)/shard_map/ppermute | solution.py:176
  134.9 3.2 %collective-permute-start.2 = (bf16[72,1152]{1,0:T(8,128)(2,1)}, bf16[72,1152]{1,0:T(8,128)(2,1)}, u32[]{:S(2)}, u32[]{:S(2)}) collective-permute-start(bf16[72,1152]{1,0:T(8,128)(2,1)} %get-tuple-element.11), channel_id=1, source_target_pairs={{0,2},{1,5},{2,8},{3,11},{4,14},{5,1},{6,4},{7,7},{8,10},{9,13},{1... | collective-permute-start | bytes 497672 | tf_op jit(solution)/shard_map/ppermute | solution.py:176
  139.7 7.5 %all-reduce = s32[24]{0:T(128)S(1)} all-reduce(s32[24]{0:T(128)S(1)} %dynamic-update-slice), channel_id=1, replica_groups=mesh['cfg'=2,'lat'=4,'seq'=16] {'lat'}, use_global_device_ids=true, to_apply=%add | all-reduce | flops 24 | bytes 192
  147.3 1.1 fusion.20
  148.5 9.4 %all-gather = bf16[4,288,24]{1,2,0:T(8,128)(2,1)S(1)} all-gather(bf16[1,288,24]{1,2,0:T(8,128)(2,1)S(1)} %fusion.20), channel_id=1, replica_groups=mesh['cfg'=2,'lat'=4,'seq'=16] {'lat'}, dimensions={0}, use_global_device_ids=true | all-gather | bytes 69120 | tf_op jit(solution)/shard_map/all_gather | solution.py:162
  159.0 3.3 %all-to-all-start = ((f32[4,6,288]{2,1,0:T(8,128)}), f32[4,6,288]{2,1,0:T(8,128)S(1)}, u32[]{:S(2)}, u32[]{:S(2)}) async-start(f32[4,6,288]{2,1,0:T(8,128)} %all_to_all.17), calls=%async_computation | async-start | bytes 98304 | tf_op jit(solution)/shard_map/all_to_all | solution.py:164
  162.5 27.0 %all_gather.30 = bf16[6,16,1024]{1,0,2:T(8,128)(2,1)} all-gather(bf16[6,16,64]{1,0,2:T(8,128)(2,1)S(1)} %copy.37), channel_id=1, replica_groups=mesh['cfg'=2,'lat'=4,'seq'=16] {'seq'}, dimensions={2}, use_global_device_ids=true | all-gather | bytes 208896 | tf_op jit(solution)/shard_map/all_gather | solution.py:172
  189.5 3.1 copy.38.lat_ref
  192.7 2.5 convolution_bitcast_fusion
  195.2 16.3 %all-gather.1 = f32[16,576,6]{1,2,0:T(8,128)S(1)} all-gather(f32[1,576,6]{1,2,0:T(8,128)S(1)} %convolution_bitcast_fusion), channel_id=1, replica_groups=mesh['cfg'=2,'lat'=4,'seq'=16] {'seq'}, dimensions={0}, use_global_device_ids=true | all-gather | bytes 235008 | tf_op jit(solution)/shard_map/all_gather | solution.py:168
  211.6 0.7 slice_add_fusion
  212.4 1.0 pad_maximum_fusion
  213.4 0.8 dynamic-slice_bitcast_fusion.1
  214.2 24.6 %shard_map.172 = bf16[6,1024,128]{2,1,0:T(8,128)(2,1)} custom-call(bf16[6,16,1024]{2,1,0:T(8,128)(2,1)} %copy.38.lat_ref, bf16[16,1152]{1,0:T(8,128)(2,1)} %patch_ref.1, f32[64,1152]{1,0:T(8,128)} %constant.82.clone.pos_ref, f32[6,1152]{1,0:T(8,128)} %get-tuple-element.19.shift_ref, f32[6,1152]{1,0:T(8,128)} %get-tuple-element.18.scale_ref, ...), custom_call_target="tpu_custom_call" | custom-call | flops 8000000000 | bytes 4000000 | tf_op jit(solution)/shard_map/pallas_call | solution.py:122
  238.8 2.8 copy.39
  241.6 5.1 %all-to-all-start.1 = ((bf16[6,16,64,72]{3,2,0,1:T(8,128)(2,1)}), bf16[6,16,64,72]{3,2,0,1:T(8,128)(2,1)}, u32[]{:S(2)}, u32[]{:S(2)}) async-start(bf16[6,16,64,72]{3,2,0,1:T(8,128)(2,1)} %copy.39), calls=%async_computation.1 | async-start | bytes 3145728 | tf_op jit(solution)/shard_map/all_to_all | solution.py:182
  246.7 0.8 constant_dynamic-slice_fusion.1
  247.5 15.4 %all-to-all-done.1 = bf16[6,16,64,72]{3,2,0,1:T(8,128)(2,1)} async-done(((bf16[6,16,64,72]{3,2,0,1:T(8,128)(2,1)}), bf16[6,16,64,72]{3,2,0,1:T(8,128)(2,1)}, u32[]{:S(2)}, u32[]{:S(2)}) %all-to-all-start.1) | async-done | bytes 884768 | tf_op jit(solution)/shard_map/all_to_all | solution.py:182
  262.9 3.6 %copy.40 = bf16[6,64,16,72]{3,2,1,0:T(8,128)(2,1)} copy(bf16[6,64,16,72]{3,1,0,2:T(8,128)(2,1)} %bitcast.18) | data formatting | bytes 1769472 | tf_op jit(solution)/shard_map/transpose | solution.py:185
  266.6 3.2 dot_general.34
  269.8 3.2 %convolution_multiply_fusion = f32[6,64,1152]{2,1,0:T(8,128)S(1)} fusion(bf16[6,64,1152]{2,1,0:T(8,128)(2,1)S(1)} %dot_general.34, bf16[1152,1152]{1,0:T(8,128)(2,1)} %all-gather.8.cloned.1.call-done, f32[6,1152]{1,0:T(8,128)} %get-tuple-element.20), kind=kOutput, calls=%fused_computation.14 | convolution fusion | flops 1019658240 | bytes 5336064 | tf_op jit(solution)/shard_map/dot_general | solution.py:41
  273.9 0.9 copy-done.1
  275.3 17.9 %fusion.8 = f32[384,1152]{1,0:T(8,128)} fusion(bf16[4608,1152]{1,0:T(8,128)(2,1)} %all-gather.16.cloned.1.call-done, bf16[384,1152]{1,0:T(8,128)(2,1)S(1)} %bitcast.64, bf16[4608,1152]{1,0:T(8,128)(2,1)} %all-gather.12.cloned.1.call-done), kind=kOutput, calls=%fused_computation.9 | convolution fusion | flops 8169652224 | bytes 23887872 | tf_op jit(solution)/shard_map/dot_general | solution.py:41
  293.2 2.4 fusion.38
  297.0 15.9 %collective-permute-start.3 = (f32[6,64,16]{1,2,0:T(8,128)S(1)}, f32[6,64,16]{1,2,0:T(8,128)S(1)}, u32[]{:S(2)}, u32[]{:S(2)}) collective-permute-start(f32[6,64,16]{1,2,0:T(8,128)S(1)} %fusion.16), channel_id=1, source_target_pairs={{0,64},{64,0},{1,65},{65,1},{2,66},{66,2},{3,67},{67,3},{4,68},{68... | collective-permute-start | bytes 73736 | tf_op jit(solution)/shard_map/ppermute | solution.py:202
  (80 shorter events, 7.1 us)
Async XLA Ops:
  6.5 186.1 %copy-start = (bf16[1001,1152]{1,0:T(8,128)(2,1)S(1)}, bf16[1001,1152]{1,0:T(8,128)(2,1)}, u32[]{:S(2)}) copy-start(bf16[1001,1152]{1,0:T(8,128)(2,1)} %param.25) | copy-start | bytes 6918916
  6.5 63.0 %all-gather.10.cloned.1.call-start = ((), (), s32[]{:S(2)}) async-start(), calls=%async_computation.3 | async-start | bytes 5640192 | tf_op jit(solution)/shard_map/all_gather | solution.py:155
  8.4 119.6 %all-gather.14.cloned.1.call-start = ((), (), s32[]{:S(2)}) async-start(), calls=%async_computation.5 | async-start | bytes 5640192 | tf_op jit(solution)/shard_map/all_gather | solution.py:156
  10.3 259.5 %all-gather.8.cloned.1.call-start = ((), (), s32[]{:S(2)}) async-start(), calls=%async_computation.2 | async-start | bytes 2820096 | tf_op jit(solution)/shard_map/all_gather | solution.py:154
  11.0 264.3 %all-gather.12.cloned.1.call-start = ((), (), s32[]{:S(2)}) async-start(), calls=%async_computation.4 | async-start | bytes 15925248 | tf_op jit(solution)/shard_map/all_gather | solution.py:155
  69.5 205.8 %all-gather.16.cloned.1.call-start = ((), (), s32[]{:S(2)}) async-start(), calls=%async_computation.6 | async-start | bytes 15925248 | tf_op jit(solution)/shard_map/all_gather | solution.py:156
  128.0 1.0 copy-start.3
  128.0 10.1 %copy-start.17 = (u32[128]{0:T(128)S(1)}, u32[128]{0:T(128)}, u32[]{:S(2)}) copy-start(u32[128]{0:T(128)} %constant.94) | copy-start | bytes 1540
  128.1 11.4 %copy-start.15 = (s32[6]{0:T(128)S(1)}, s32[6]{0:T(128)}, u32[]{:S(2)}) copy-start(s32[6]{0:T(128)} %param.19) | copy-start | bytes 76
  128.1 30.0 %copy-start.2 = (bf16[1152,288]{0,1:T(8,128)(2,1)S(1)}, bf16[1152,288]{0,1:T(8,128)(2,1)}, u32[]{:S(2)}) copy-start(bf16[1152,288]{0,1:T(8,128)(2,1)} %param.27) | copy-start | bytes 1990660
  128.1 34.2 %copy-start.4 = (f32[6,64,16]{1,2,0:T(8,128)S(1)}, f32[6,64,16]{1,2,0:T(8,128)}, u32[]{:S(2)}) copy-start(f32[6,64,16]{1,2,0:T(8,128)} %param.18) | copy-start | bytes 73732
  128.1 34.3 %copy-start.16 = (s32[6]{0:T(128)S(1)}, s32[6]{0:T(128)}, u32[]{:S(2)}) copy-start(s32[6]{0:T(128)} %param.20) | copy-start | bytes 76
  129.9 82.5 %collective-permute-start = (bf16[72,1152]{1,0:T(8,128)(2,1)}, bf16[72,1152]{1,0:T(8,128)(2,1)S(1)}, u32[]{:S(2)}, u32[]{:S(2)}) collective-permute-start(bf16[72,1152]{1,0:T(8,128)(2,1)} %get-tuple-element.10), channel_id=1, source_target_pairs={{0,0},{1,3},{2,6},{3,9},{4,12},{5,15},{6,2},{7,5},{8,8},{9,11},{10... | collective-permute-start | bytes 497672 | tf_op jit(solution)/shard_map/ppermute | solution.py:176
  131.5 80.9 %collective-permute-start.1 = (bf16[72,1152]{1,0:T(8,128)(2,1)}, bf16[72,1152]{1,0:T(8,128)(2,1)S(1)}, u32[]{:S(2)}, u32[]{:S(2)}) collective-permute-start(bf16[72,1152]{1,0:T(8,128)(2,1)} %get-tuple-element.12), channel_id=1, source_target_pairs={{0,1},{1,4},{2,7},{3,10},{4,13},{5,0},{6,3},{7,6},{8,9},{9,12},{10... | collective-permute-start | bytes 497672 | tf_op jit(solution)/shard_map/ppermute | solution.py:176
  134.9 77.5 %collective-permute-start.2 = (bf16[72,1152]{1,0:T(8,128)(2,1)}, bf16[72,1152]{1,0:T(8,128)(2,1)}, u32[]{:S(2)}, u32[]{:S(2)}) collective-permute-start(bf16[72,1152]{1,0:T(8,128)(2,1)} %get-tuple-element.11), channel_id=1, source_target_pairs={{0,2},{1,5},{2,8},{3,11},{4,14},{5,1},{6,4},{7,7},{8,10},{9,13},{1... | collective-permute-start | bytes 497672 | tf_op jit(solution)/shard_map/ppermute | solution.py:176
  159.0 33.6 %all-to-all-start = ((f32[4,6,288]{2,1,0:T(8,128)}), f32[4,6,288]{2,1,0:T(8,128)S(1)}, u32[]{:S(2)}, u32[]{:S(2)}) async-start(f32[4,6,288]{2,1,0:T(8,128)} %all_to_all.17), calls=%async_computation | async-start | bytes 98304 | tf_op jit(solution)/shard_map/all_to_all | solution.py:164
  241.6 5.9 %copy-start.5 = (f32[32,1152]{1,0:T(8,128)S(1)}, f32[32,1152]{1,0:T(8,128)}, u32[]{:S(2)}) copy-start(f32[32,1152]{1,0:T(8,128)} %constant.91) | copy-start | bytes 442372
  241.6 21.4 %all-to-all-start.1 = ((bf16[6,16,64,72]{3,2,0,1:T(8,128)(2,1)}), bf16[6,16,64,72]{3,2,0,1:T(8,128)(2,1)}, u32[]{:S(2)}, u32[]{:S(2)}) async-start(bf16[6,16,64,72]{3,2,0,1:T(8,128)(2,1)} %copy.39), calls=%async_computation.1 | async-start | bytes 3145728 | tf_op jit(solution)/shard_map/all_to_all | solution.py:182
  269.8 3.2 %copy-start.11 = (bf16[16,1152]{1,0:T(8,128)(2,1)S(1)}, bf16[16,1152]{1,0:T(8,128)(2,1)}, u32[]{:S(2)}) copy-start(bf16[16,1152]{1,0:T(8,128)(2,1)} %patch_ref.1) | copy-start | bytes 110596
  273.6 1.2 copy-start.1
  273.6 1.2 copy-start.6
  273.6 1.2 copy-start.7
  275.3 17.9 %copy-start.8 = (f32[6,1152]{1,0:T(8,128)S(1)}, f32[6,1152]{1,0:T(8,128)}, u32[]{:S(2)}) copy-start(f32[6,1152]{1,0:T(8,128)} %get-tuple-element.17) | copy-start | bytes 82948
  295.6 0.8 copy-start.9
  295.6 0.8 copy-start.10
  295.6 0.8 copy-start.14
  295.6 18.2 %copy-start.12 = (f32[6]{0:T(128)S(1)}, f32[6]{0:T(128)}, u32[]{:S(2)}) copy-start(f32[6]{0:T(128)} %param.23) | copy-start | bytes 76
  295.6 18.2 %copy-start.13 = (f32[6]{0:T(128)S(1)}, f32[6]{0:T(128)}, u32[]{:S(2)}) copy-start(f32[6]{0:T(128)} %param.22) | copy-start | bytes 76
  297.0 16.8 %collective-permute-start.3 = (f32[6,64,16]{1,2,0:T(8,128)S(1)}, f32[6,64,16]{1,2,0:T(8,128)S(1)}, u32[]{:S(2)}, u32[]{:S(2)}) collective-permute-start(f32[6,64,16]{1,2,0:T(8,128)S(1)} %fusion.16), channel_id=1, source_target_pairs={{0,64},{64,0},{1,65},{65,1},{2,66},{66,2},{3,67},{67,3},{4,68},{68... | collective-permute-start | bytes 73736 | tf_op jit(solution)/shard_map/ppermute | solution.py:202
Sparse Core Ops, SparseCore 0:
  9.5 59.9 all-gather.9
  71.7 56.3 all-gather.13
  130.2 48.8 all-gather.7
  180.6 25.1 all-gather.11
  207.4 27.0 all-gather.15

commit v2 on v1

--- a/solution.py
+++ b/solution.py
@@ -23,6 +23,7 @@
 BF16 = jnp.bfloat16
 NT = (((1,), (1,)), ((), ()))
 NN = (((1,), (0,)), ((), ()))
+MESH = pl.DeviceIdType.MESH
 HIGH = lax.Precision.HIGHEST
 
 
@@ -141,6 +142,82 @@
     )(lat, patch, centred, shift, scale, wq, wk, wv)
 
 
+def feed_forward_kernel(
+    guidance_ref, state_ref, shift_ref, scale_ref, gate_ref, last_shift_ref, last_scale_ref, fc1_ref, fc2_ref, out_w_ref,
+    out_ref, normed_ref, total_ref, noise_ref, partner_ref, send_sem, recv_sem,
+):
+    step = pl.program_id(0)
+    side = lax.axis_index("cfg")
+    count = shift_ref.shape[0]
+    tokens = state_ref.shape[0] // count
+    barrier = pltpu.get_barrier_semaphore()
+
+    @pl.when(step == 0)
+    def _():
+        pl.semaphore_signal(barrier, inc=1, device_id={"cfg": 1 - side}, device_id_type=MESH)
+        for l in range(count):
+            rows = slice(l * tokens, (l + 1) * tokens)
+            normed_ref[rows, :] = (
+                layer_norm(state_ref[rows, :]) * (1.0 + scale_ref[l : l + 1, :]) + shift_ref[l : l + 1, :]
+            ).astype(BF16)
+        total_ref[...] = jnp.zeros_like(total_ref)
+
+    units = fc1_ref.shape[0] * fc1_ref.shape[1]
+    hidden = dot(normed_ref[...], fc1_ref[...].reshape(units, D), NT)
+    hidden = jax.nn.gelu(hidden, approximate=True).astype(BF16)
+    total_ref[...] += dot(hidden, fc2_ref[...].reshape(units, D))
+
+    @pl.when(step == pl.num_programs(0) - 1)
+    def _():
+        for l in range(count):
+            rows = slice(l * tokens, (l + 1) * tokens)
+            state = state_ref[rows, :] + gate_ref[l : l + 1, :] * total_ref[rows, :]
+            normed_ref[rows, :] = (
+                layer_norm(state) * (1.0 + last_scale_ref[l : l + 1, :]) + last_shift_ref[l : l + 1, :]
+            ).astype(BF16)
+        noise_ref[...] = dot(out_w_ref[...], normed_ref[...], (((0,), (1,)), ((), ())))
+        pl.semaphore_wait(barrier, 1)
+        copy = pltpu.make_async_remote_copy(
+            src_ref=noise_ref.at[pl.ds(pl.multiple_of((1 - side) * 8, 8), 8)],
+            dst_ref=partner_ref,
+            send_sem=send_sem,
+            recv_sem=recv_sem,
+            device_id={"cfg": 1 - side},
+            device_id_type=MESH,
+        )
+        copy.start()
+        copy.wait()
+        own = noise_ref[pl.ds(pl.multiple_of(side * 8, 8), 8), :]
+        cond_noise = jnp.where(side == 0, own, partner_ref[...])
+        free_noise = jnp.where(side == 0, partner_ref[...], own)
+        out_ref[...] = free_noise + guidance_ref[0] * (cond_noise - free_noise)
+
+
+def feed_forward(state, pieces, stacked, w_out, guidance, rows):
+    tokens = state.shape[0]
+    shift, scale, gate, last_shift, last_scale = pieces
+    whole = pl.BlockSpec(memory_space=pltpu.VMEM)
+    group = 4
+    weights = [pl.BlockSpec((group, rows, D), lambda i, b=b: (i, b, 0)) for b in range(2)]
+    return pl.pallas_call(
+        feed_forward_kernel,
+        grid=(stacked.shape[0] // group,),
+        out_shape=jax.ShapeDtypeStruct((8, tokens), F32),
+        in_specs=[pl.BlockSpec(memory_space=pltpu.SMEM)] + [whole] * 6 + weights + [whole],
+        out_specs=whole,
+        scratch_shapes=[
+            pltpu.VMEM((tokens, D), BF16),
+            pltpu.VMEM((tokens, D), F32),
+            pltpu.VMEM((16, tokens), F32),
+            pltpu.VMEM((8, tokens), F32),
+            pltpu.SemaphoreType.DMA,
+            pltpu.SemaphoreType.DMA,
+        ],
+        compiler_params=pltpu.CompilerParams(collective_id=0, has_side_effects=True),
+        cost_estimate=pl.CostEstimate(flops=8 * 10**9, bytes_accessed=24 * 10**6, transcendentals=2 * 10**6),
+    )(guidance, state, shift, scale, gate, last_shift, last_scale, stacked, stacked, w_out)
+
+
 def shards(
     latents, timesteps, labels, guidance, keep_coef, noise_coef, w_patch, label_table,
     w_time1, w_time2, ada_weight, w_qkv, w_proj, w_fc1, w_fc2, w_out,
@@ -148,12 +225,9 @@
     count, tok_count, channels = latents.shape
     side = lax.axis_index("cfg")
     place = lax.axis_index("seq")
-    half = w_fc2.shape[0] // 2
-    fc1_half = lax.dynamic_slice_in_dim(w_fc1.T, side * half, half, 0)
-    fc2_half = lax.dynamic_slice_in_dim(w_fc2, side * half, half, 0)
-    proj_full = lax.all_gather(w_proj.T, "seq", axis=0, tiled=True)
-    fc1_full = lax.all_gather(lax.all_gather(fc1_half, "seq", axis=0, tiled=True), "cfg", axis=0, tiled=True)
-    fc2_full = lax.all_gather(lax.all_gather(fc2_half, "seq", axis=0, tiled=True), "cfg", axis=0, tiled=True)
+    rows = w_fc2.shape[0]
+    stacked = lax.all_gather(jnp.concatenate([w_fc1.T, w_fc2, w_proj.T], axis=0), "seq", axis=0)
+    proj_full = stacked[:, 2 * rows :].reshape(D, D)
 
     classes = jnp.where(side == 0, labels, CLASSES)
     steps_all = lax.all_gather(timesteps, "lat", axis=0, tiled=True)
@@ -191,19 +265,10 @@
     state = dot(latents.reshape(-1, channels).astype(BF16), w_patch).reshape(count, tok_count, D) + own_pos[None]
     projected = dot(attended, proj_full, NT).reshape(count, tok_count, D)
     state = state + pieces[2][:, None, :] * projected
-    normed = (layer_norm(state) * (1.0 + pieces[4][:, None, :]) + pieces[3][:, None, :]).astype(BF16).reshape(-1, D)
-    hidden = jax.nn.gelu(dot(normed, fc1_full, NT), approximate=True).astype(BF16)
-    mlp_out = dot(hidden, fc2_full).reshape(count, tok_count, D)
-    state = state + pieces[5][:, None, :] * mlp_out
-    final = (layer_norm(state) * (1.0 + pieces[7][:, None, :]) + pieces[6][:, None, :]).astype(BF16).reshape(-1, D)
-    noise_own = dot(final, w_out).reshape(count, tok_count, channels)
+    guided = feed_forward(state.reshape(-1, D), pieces[3:], stacked, w_out, guidance, rows)
     half_width = channels // 2
     own_latent = lax.dynamic_slice_in_dim(latents, side * half_width, half_width, 2)
-    partner = lax.ppermute(noise_own, "cfg", [(0, 1), (1, 0)])
-    cond_noise = jnp.where(side == 0, noise_own, partner)
-    free_noise = jnp.where(side == 0, partner, noise_own)
-    combined = free_noise + guidance[0] * (cond_noise - free_noise)
-    guided = lax.dynamic_slice_in_dim(combined, side * half_width, half_width, 2)
+    guided = guided.T.reshape(count, tok_count, half_width)
     return keep_coef[:, None, None] * own_latent + noise_coef[:, None, None] * guided
 
 

time: 322 us -> 225 us (0.70)
  waiting for transfers between devices: 133 us -> 41.3 us
  Pallas kernels: 24.6 us -> 46.1 us
  matrix products: 26.1 us -> 6.73 us
  starting transfers between devices: 32.7 us -> 18.9 us
  blocking collectives: 60.2 us -> 69.6 us
    all_gather x5 -> x1, waiting for transfers between devices: 117 us -> 8.77 us  [shards(): lax.all_gather(jnp.concatenate([w_fc1.T, w_fc2, w_proj.T], axis=0), 'seq'...]
    pallas_call x0 -> x1, Pallas kernels: none -> 21.4 us  [feed_forward(): pl.pallas_call(feed_forward_kernel, grid=(stacked.shape[0] // group,), ou...]
    dot_general x7 -> x5, matrix products: 26.1 us -> 6.73 us  [dot(): lax.dot_general(a, b, dims, precision=precision, preferred_element_type=F32)]
    all_to_all x1, waiting for transfers between devices: 15.4 us -> 32.5 us  [shards(): lax.all_to_all(attended[:, :, :HEAD_DIM].reshape(count, HEADS, tok_count,...]
    ppermute x1 -> x0, starting transfers between devices: 15.9 us -> none  [shards(): partner = lax.ppermute(noise_own, 'cfg', [(0, 1), (1, 0)])]
    all_gather x1, blocking collectives: 27 us -> 31.4 us  [shards(): lat_all = lax.all_gather(lat_t, 'seq', axis=2, tiled=True)]
    all_gather x1, blocking collectives: 16.3 us -> 20.7 us  [shards(): modulation = lax.all_gather(own_columns, 'seq', axis=1, tiled=True)]
  transfers between devices with their start and end apart: 11 -> 6, of which waited for: 4 -> 2; matrix products, arithmetic and copies ran while one was open for 9% -> 10% of each run, Pallas kernels for 8% -> 11%
where the time goes in v2:
time: 225 us; the launch traced here: 224 us
  blocking collectives  69.6 us (31%)
  Pallas kernels  46.1 us (20%)
  waiting for transfers between devices  41.3 us (18%)
  local copies, waits for them, and re-layouts  22.4 us (10%)
  starting transfers between devices  18.9 us (8%)
  between operations  15 us (7%)
  matrix products  6.73 us (3%)
  other arithmetic  3.99 us (2%)
    all_to_all x1, waiting for transfers between devices, shards(): lax.all_to_all(attended[:, :, :HEAD_DIM].reshape(count, HEADS, tok_count,...  32.5 us
    all_gather x1, blocking collectives, shards(): lat_all = lax.all_gather(lat_t, 'seq', axis=2, tiled=True)  31.4 us
    pallas_call x1, Pallas kernels, attend(): pl.pallas_call(attend_kernel, out_shape=jax.ShapeDtypeStruct((count, TOKE...  24.7 us
    pallas_call x1, Pallas kernels, feed_forward(): pl.pallas_call(feed_forward_kernel, grid=(stacked.shape[0] // group,), ou...  21.4 us
    all_gather x1, blocking collectives, shards(): modulation = lax.all_gather(own_columns, 'seq', axis=1, tiled=True)  20.7 us
    ppermute x3, starting transfers between devices, shards(): lax.ppermute(blocks[j], 'seq', [(s, (3 * s + j) % HEADS) for s in range(H...  10.9 us
    all_gather x1, blocking collectives, shards(): hidden_time = lax.all_gather(hidden_own, 'lat', axis=1, tiled=True)  10.2 us
    all_gather x1, waiting for transfers between devices, shards(): lax.all_gather(jnp.concatenate([w_fc1.T, w_fc2, w_proj.T], axis=0), 'seq'...  8.77 us
  transfers between devices with their start and end apart: 6, of which 2 were waited for; matrix products, arithmetic and copies ran while one was open for 10% of the time, Pallas kernels for 11%

profile of v2, /device:TPU:1, one launch (start us, length us, event | category | flops | bytes accessed | tf_op | source)
XLA Modules:
  0.0 224.0 jit_solution(14979753779375584521)
XLA Ops:
  6.5 2.7 %pad_maximum_fusion = bf16[648,1152]{1,0:T(8,128)(2,1)} fusion(bf16[72,1152]{1,0:T(8,128)(2,1)} %bitcast.64, bf16[288,1152]{1,0:T(8,128)(2,1)} %param.32, bf16[288,1152]{1,0:T(8,128)(2,1)} %bitcast.61), kind=kLoop, calls=%fused_computation.4 | loop fusion | flops 4478976 | bytes 2985984 | tf_op jit(solution)/shard_map/concatenate | solution.py:229
  9.4 0.8 fusion.18
  10.2 1.6 collective-permute-start
  11.7 4.6 %collective-permute-start.1 = (bf16[72,1152]{1,0:T(8,128)(2,1)}, bf16[72,1152]{1,0:T(8,128)(2,1)S(1)}, u32[]{:S(2)}, u32[]{:S(2)}) collective-permute-start(bf16[72,1152]{1,0:T(8,128)(2,1)} %get-tuple-element.10), channel_id=1, source_target_pairs={{0,1},{1,4},{2,7},{3,10},{4,13},{5,0},{6,3},{7,6},{8,9},{9,12},{10... | collective-permute-start | bytes 497672 | tf_op jit(solution)/shard_map/ppermute | solution.py:250
  16.3 4.8 %collective-permute-start.2 = (bf16[72,1152]{1,0:T(8,128)(2,1)}, bf16[72,1152]{1,0:T(8,128)(2,1)}, u32[]{:S(2)}, u32[]{:S(2)}) collective-permute-start(bf16[72,1152]{1,0:T(8,128)(2,1)} %get-tuple-element.9), channel_id=1, source_target_pairs={{0,2},{1,5},{2,8},{3,11},{4,14},{5,1},{6,4},{7,7},{8,10},{9,13},{1... | collective-permute-start | bytes 497672 | tf_op jit(solution)/shard_map/ppermute | solution.py:250
  22.6 7.3 %all-reduce = s32[24]{0:T(128)S(1)} all-reduce(s32[24]{0:T(128)S(1)} %dynamic-update-slice), channel_id=1, replica_groups=mesh['cfg'=2,'lat'=4,'seq'=16] {'lat'}, use_global_device_ids=true, to_apply=%add | all-reduce | flops 24 | bytes 192
  30.0 1.1 fusion.4
  31.1 10.2 %all-gather.1 = bf16[4,288,24]{1,2,0:T(8,128)(2,1)S(1)} all-gather(bf16[1,288,24]{1,2,0:T(8,128)(2,1)S(1)} %fusion.4), channel_id=1, replica_groups=mesh['cfg'=2,'lat'=4,'seq'=16] {'lat'}, dimensions={0}, use_global_device_ids=true | all-gather | bytes 69120 | tf_op jit(solution)/shard_map/all_gather | solution.py:236
  41.8 0.7 all_to_all.17
  42.5 3.3 %all-to-all-start = ((f32[4,6,288]{2,1,0:T(8,128)}), f32[4,6,288]{2,1,0:T(8,128)S(1)}, u32[]{:S(2)}, u32[]{:S(2)}) async-start(f32[4,6,288]{2,1,0:T(8,128)} %all_to_all.17), calls=%async_computation | async-start | bytes 98304 | tf_op jit(solution)/shard_map/all_to_all | solution.py:238
  45.9 31.4 %all_gather.21 = bf16[6,16,1024]{1,0,2:T(8,128)(2,1)} all-gather(bf16[6,16,64]{1,0,2:T(8,128)(2,1)S(1)} %copy.46), channel_id=1, replica_groups=mesh['cfg'=2,'lat'=4,'seq'=16] {'seq'}, dimensions={2}, use_global_device_ids=true | all-gather | bytes 208896 | tf_op jit(solution)/shard_map/all_gather | solution.py:246
  77.4 2.9 %copy.47.lat_ref = bf16[6,16,1024]{2,1,0:T(8,128)(2,1)} copy(bf16[6,16,1024]{1,0,2:T(8,128)(2,1)} %all_gather.21) | data formatting | bytes 393216 | tf_op jit(solution)/shard_map/all_gather | solution.py:246
  80.4 2.2 convolution_bitcast_fusion
  82.6 20.7 %all-gather.2 = f32[16,576,6]{1,2,0:T(8,128)S(1)} all-gather(f32[1,576,6]{1,2,0:T(8,128)S(1)} %convolution_bitcast_fusion), channel_id=1, replica_groups=mesh['cfg'=2,'lat'=4,'seq'=16] {'seq'}, dimensions={0}, use_global_device_ids=true | all-gather | bytes 235008 | tf_op jit(solution)/shard_map/all_gather | solution.py:242
  103.5 0.8 fusion.19
  104.2 1.0 pad_maximum_fusion.1
  105.2 0.8 dynamic-slice_bitcast_fusion
  106.1 24.7 %shard_map.172 = bf16[6,1024,128]{2,1,0:T(8,128)(2,1)} custom-call(bf16[6,16,1024]{2,1,0:T(8,128)(2,1)} %copy.47.lat_ref, bf16[16,1152]{1,0:T(8,128)(2,1)} %patch_ref.1, f32[64,1152]{1,0:T(8,128)} %constant.60.clone.pos_ref, f32[6,1152]{1,0:T(8,128)} %get-tuple-element.17.shift_ref, f32[6,1152]{1,0:T(8,128)} %get-tuple-element.16.scale_ref, ...), custom_call_target="tpu_custom_call" | custom-call | flops 8000000000 | bytes 4000000 | tf_op jit(solution)/shard_map/pallas_call | solution.py:123
  130.8 2.7 %copy.48 = bf16[6,16,64,72]{3,2,0,1:T(8,128)(2,1)} copy(bf16[6,16,64,72]{3,2,1,0:T(8,128)(2,1)} %bitcast.58) | data formatting | bytes 1769472 | tf_op jit(solution)/shard_map/reshape | solution.py:257
  133.5 4.7 %all-to-all-start.1 = ((bf16[6,16,64,72]{3,2,0,1:T(8,128)(2,1)}), bf16[6,16,64,72]{3,2,0,1:T(8,128)(2,1)}, u32[]{:S(2)}, u32[]{:S(2)}) async-start(bf16[6,16,64,72]{3,2,0,1:T(8,128)(2,1)} %copy.48), calls=%async_computation.1 | async-start | bytes 3145728 | tf_op jit(solution)/shard_map/all_to_all | solution.py:256
  138.3 0.9 copy.50.out_w_ref
  139.8 0.6 constant_dynamic-slice_fusion.1
  140.4 0.8 constant_dynamic-slice_fusion
  141.2 32.5 %all-to-all-done.1 = bf16[6,16,64,72]{3,2,0,1:T(8,128)(2,1)} async-done(((bf16[6,16,64,72]{3,2,0,1:T(8,128)(2,1)}), bf16[6,16,64,72]{3,2,0,1:T(8,128)(2,1)}, u32[]{:S(2)}, u32[]{:S(2)}) %all-to-all-start.1) | async-done | bytes 884768 | tf_op jit(solution)/shard_map/all_to_all | solution.py:256
  173.7 3.6 %copy.49 = bf16[6,64,16,72]{3,2,1,0:T(8,128)(2,1)} copy(bf16[6,64,16,72]{3,1,0,2:T(8,128)(2,1)} %bitcast.18) | data formatting | bytes 1769472 | tf_op jit(solution)/shard_map/transpose | solution.py:259
  177.3 3.0 %dot_general.25 = bf16[6,64,1152]{2,1,0:T(8,128)(2,1)S(1)} reshape(bf16[6,64,16,72]{3,2,1,0:T(8,128)(2,1)} %copy.49) | data formatting | bytes 1769472 | tf_op jit(solution)/shard_map/dot_general | solution.py:42
  180.3 8.8 %all-gather.5.cloned.1.call-done = bf16[10368,1152]{1,0:T(8,128)(2,1)} async-done(((bf16[648,1152]{1,0:T(8,128)(2,1)}), bf16[10368,1152]{1,0:T(8,128)(2,1)}) %all-gather.5.cloned.1.call-update) | async-done | bytes 23887888 | tf_op jit(solution)/shard_map/all_gather | solution.py:229
  189.1 2.0 slice.66
  191.1 1.5 convolution_multiply_fusion
  192.6 1.7 fusion
  194.3 21.4 %shard_map.173 = f32[8,384]{1,0:T(8,128)} custom-call(f32[1]{0:T(128)S(6)} %copy.57.guidance_ref, f32[384,1152]{1,0:T(8,128)} %bitcast.56, f32[6,1152]{1,0:T(8,128)} %get-tuple-element.15.shift_ref, f32[6,1152]{1,0:T(8,128)} %get-tuple-element.14.scale_ref, f32[6,1152]{1,0:T(8,128)} %get-tuple-element.13.gate_ref, ...), custom_call_target="tpu_custom_call" | custom-call | flops 8000000000 | bytes 24000000 | tf_op jit(solution)/shard_map/pallas_call | solution.py:202
  215.7 0.8 reshape.58
  (53 shorter events, 2.6 us)
Async XLA Ops:
  6.5 73.9 %copy-start = (bf16[1001,1152]{1,0:T(8,128)(2,1)S(1)}, bf16[1001,1152]{1,0:T(8,128)(2,1)}, u32[]{:S(2)}) copy-start(bf16[1001,1152]{1,0:T(8,128)(2,1)} %param.25) | copy-start | bytes 6918916
  6.5 182.6 %all-gather.5.cloned.1.call-start = ((), (), s32[]{:S(2)}) async-start(), calls=%async_computation.2 | async-start | bytes 25380864 | tf_op jit(solution)/shard_map/all_gather | solution.py:229
  6.5 2.8 %copy-start.2 = (bf16[1152,216]{0,1:T(8,128)(2,1)S(1)}, bf16[1152,216]{0,1:T(8,128)(2,1)}, u32[]{:S(2)}) copy-start(bf16[1152,216]{0,1:T(8,128)(2,1)} %param.29) | copy-start | bytes 1492996
  9.3 11.8 %copy-start.13 = (u32[128]{0:T(128)S(1)}, u32[128]{0:T(128)}, u32[]{:S(2)}) copy-start(u32[128]{0:T(128)} %constant.72) | copy-start | bytes 1540
  9.3 13.1 %copy-start.11 = (s32[6]{0:T(128)S(1)}, s32[6]{0:T(128)}, u32[]{:S(2)}) copy-start(s32[6]{0:T(128)} %param.19) | copy-start | bytes 76
  9.3 32.2 %copy-start.1 = (bf16[1152,288]{0,1:T(8,128)(2,1)S(1)}, bf16[1152,288]{0,1:T(8,128)(2,1)}, u32[]{:S(2)}) copy-start(bf16[1152,288]{0,1:T(8,128)(2,1)} %param.27) | copy-start | bytes 1990660
  9.3 36.5 %copy-start.3 = (f32[6,64,16]{1,2,0:T(8,128)S(1)}, f32[6,64,16]{1,2,0:T(8,128)}, u32[]{:S(2)}) copy-start(f32[6,64,16]{1,2,0:T(8,128)} %param.18) | copy-start | bytes 73732
  9.3 36.6 %copy-start.12 = (s32[6]{0:T(128)S(1)}, s32[6]{0:T(128)}, u32[]{:S(2)}) copy-start(s32[6]{0:T(128)} %param.20) | copy-start | bytes 76
  10.2 94.1 %collective-permute-start = (bf16[72,1152]{1,0:T(8,128)(2,1)}, bf16[72,1152]{1,0:T(8,128)(2,1)S(1)}, u32[]{:S(2)}, u32[]{:S(2)}) collective-permute-start(bf16[72,1152]{1,0:T(8,128)(2,1)} %get-tuple-element.8), channel_id=1, source_target_pairs={{0,0},{1,3},{2,6},{3,9},{4,12},{5,15},{6,2},{7,5},{8,8},{9,11},{10... | collective-permute-start | bytes 497672 | tf_op jit(solution)/shard_map/ppermute | solution.py:250
  11.7 92.5 %collective-permute-start.1 = (bf16[72,1152]{1,0:T(8,128)(2,1)}, bf16[72,1152]{1,0:T(8,128)(2,1)S(1)}, u32[]{:S(2)}, u32[]{:S(2)}) collective-permute-start(bf16[72,1152]{1,0:T(8,128)(2,1)} %get-tuple-element.10), channel_id=1, source_target_pairs={{0,1},{1,4},{2,7},{3,10},{4,13},{5,0},{6,3},{7,6},{8,9},{9,12},{10... | collective-permute-start | bytes 497672 | tf_op jit(solution)/shard_map/ppermute | solution.py:250
  16.3 87.9 %collective-permute-start.2 = (bf16[72,1152]{1,0:T(8,128)(2,1)}, bf16[72,1152]{1,0:T(8,128)(2,1)}, u32[]{:S(2)}, u32[]{:S(2)}) collective-permute-start(bf16[72,1152]{1,0:T(8,128)(2,1)} %get-tuple-element.9), channel_id=1, source_target_pairs={{0,2},{1,5},{2,8},{3,11},{4,14},{5,1},{6,4},{7,7},{8,10},{9,13},{1... | collective-permute-start | bytes 497672 | tf_op jit(solution)/shard_map/ppermute | solution.py:250
  42.5 37.8 %all-to-all-start = ((f32[4,6,288]{2,1,0:T(8,128)}), f32[4,6,288]{2,1,0:T(8,128)S(1)}, u32[]{:S(2)}, u32[]{:S(2)}) async-start(f32[4,6,288]{2,1,0:T(8,128)} %all_to_all.17), calls=%async_computation | async-start | bytes 98304 | tf_op jit(solution)/shard_map/all_to_all | solution.py:238
  133.5 4.7 %copy-start.8 = (bf16[1152,16]{0,1:T(8,128)(2,1)S(1)}, bf16[1152,16]{0,1:T(8,128)(2,1)}, u32[]{:S(2)}) copy-start(bf16[1152,16]{0,1:T(8,128)(2,1)} %param.33) | copy-start | bytes 110596
  133.5 7.7 %copy-start.4 = (f32[32,1152]{1,0:T(8,128)S(1)}, f32[32,1152]{1,0:T(8,128)}, u32[]{:S(2)}) copy-start(f32[32,1152]{1,0:T(8,128)} %constant.69) | copy-start | bytes 442372
  133.5 40.2 %all-to-all-start.1 = ((bf16[6,16,64,72]{3,2,0,1:T(8,128)(2,1)}), bf16[6,16,64,72]{3,2,0,1:T(8,128)(2,1)}, u32[]{:S(2)}, u32[]{:S(2)}) async-start(bf16[6,16,64,72]{3,2,0,1:T(8,128)(2,1)} %copy.48), calls=%async_computation.1 | async-start | bytes 3145728 | tf_op jit(solution)/shard_map/all_to_all | solution.py:256
  189.1 2.0 copy-start.7
  191.1 1.5 copy-start.6
  194.3 22.2 %copy-start.5 = (f32[6,64,8]{1,2,0:T(8,128)S(1)}, f32[6,64,8]{1,2,0:T(8,128)}, u32[]{:S(2)}) copy-start(f32[6,64,8]{1,2,0:T(8,128)} %constant_dynamic-slice_fusion.1) | copy-start | bytes 36868
  194.3 22.2 %copy-start.9 = (f32[6]{0:T(128)S(1)}, f32[6]{0:T(128)}, u32[]{:S(2)}) copy-start(f32[6]{0:T(128)} %param.23) | copy-start | bytes 76
  194.3 22.2 %copy-start.10 = (f32[6]{0:T(128)S(1)}, f32[6]{0:T(128)}, u32[]{:S(2)}) copy-start(f32[6]{0:T(128)} %param.22) | copy-start | bytes 76
Sparse Core Ops, SparseCore 0:
  9.5 179.5 all-gather.4

commit v3 on v2

--- a/solution.py
+++ b/solution.py
@@ -56,11 +56,44 @@
     return jnp.concatenate([jnp.cos(angles), jnp.sin(angles)], axis=-1)
 
 
+def ring(me, body):
+    def one(k, carry):
+        body(k, lax.rem(me + k, HEADS))
+        return carry
+
+    lax.fori_loop(1, HEADS, one, 0)
+
+
+def remote(source, target, send_sem, recv_sem, peer):
+    return pltpu.make_async_remote_copy(
+        src_ref=source, dst_ref=target, send_sem=send_sem, recv_sem=recv_sem, device_id=peer, device_id_type=MESH
+    )
+
+
 def attend_kernel(
-    lat_ref, patch_ref, pos_ref, shift_ref, scale_ref, wq_ref, wk_ref, wv_ref,
-    out_ref, ft_ref, base_ref, xs_ref, tq_ref, tv_ref, tk_ref, rstd_ref, rcol_ref, q_ref, v_ref, kt_ref,
+    lat_ref, cols_ref, patch_ref, pos_ref, wq_ref, wk_ref, wv_ref,
+    out_ref, mods_ref,
+    lat_all, cols_all, arrived, own_ref, lat_send, lat_recv, cols_send, cols_recv, out_send, out_recv,
+    ft_ref, base_ref, xs_ref, tq_ref, tv_ref, tk_ref, rstd_ref, rcol_ref, q_ref, v_ref, kt_ref,
 ):
     count = lat_ref.shape[0]
+    tokens = lat_ref.shape[2]
+    me = lax.axis_index("seq")
+    barrier = pltpu.get_barrier_semaphore()
+    ring(me, lambda k, peer: pl.semaphore_signal(barrier, inc=1, device_id={"seq": peer}, device_id_type=MESH))
+    pl.semaphore_wait(barrier, HEADS - 1)
+
+    def send_inputs(k, peer):
+        remote(cols_ref, cols_all.at[me], cols_send.at[k], cols_recv.at[me], {"seq": peer}).start()
+        remote(lat_ref, lat_all.at[me], lat_send.at[k], lat_recv.at[me], {"seq": peer}).start()
+
+    def wait_inputs(k, peer):
+        remote(cols_ref, cols_all.at[peer], cols_send.at[k], cols_recv.at[peer], {"seq": peer}).wait()
+        remote(lat_ref, lat_all.at[peer], lat_send.at[k], lat_recv.at[peer], {"seq": peer}).wait()
+
+    ring(me, send_inputs)
+    lat_all[me] = lat_ref[...]
+    cols_all[me] = cols_ref[...]
     patch = patch_ref[...].astype(F32)
     base_ref[:16, :] = patch - jnp.mean(patch, axis=1, keepdims=True)
     base_ref[16:, :] = pos_ref[...]
@@ -70,15 +103,20 @@
     place = lax.broadcasted_iota(jnp.int32, (2 * GRID, TOKENS), 0)
     hot = jnp.where(jnp.where(place < GRID, token % GRID, token // GRID + GRID) == place, 1.0, 0.0).astype(BF16)
     rstd_ref[...] = jnp.zeros_like(rstd_ref)
+    ring(me, wait_inputs)
+    for n in range(8):
+        mods_ref[n] = jnp.concatenate([cols_all[2 * n], cols_all[2 * n + 1]], axis=1)
     for l in range(count):
-        ft_ref[l, :16, :] = lat_ref[l]
+        for n in range(HEADS // 2):
+            pair = [lat_all[2 * n + m, l].astype(F32) for m in range(2)]
+            ft_ref[l, :16, n * LANES : (n + 1) * LANES] = jnp.concatenate(pair, axis=1).astype(BF16)
         ft_ref[l, 16:, :] = hot
         ft = ft_ref[l].astype(F32)
         spread = jnp.sum(dot(gram, ft, NN, HIGH) * ft, axis=0, keepdims=True)
         rstd_ref[l : l + 1, :] = lax.rsqrt(spread + 1e-06)
-        xs_ref[l * ROWS : l * ROWS + BASE, :] = (base * (1.0 + scale_ref[l : l + 1, :])).astype(BF16)
+        xs_ref[l * ROWS : l * ROWS + BASE, :] = (base * (1.0 + mods_ref[1, l : l + 1, :])).astype(BF16)
         xs_ref[l * ROWS + BASE : (l + 1) * ROWS, :] = jnp.broadcast_to(
-            shift_ref[l : l + 1, :], (ROWS - BASE, D)
+            mods_ref[0, l : l + 1, :], (ROWS - BASE, D)
         ).astype(BF16)
     rcol_ref[...] = jnp.transpose(rstd_ref[...])
     factor = math.log2(math.e) / math.sqrt(HEAD_DIM)
@@ -108,24 +146,56 @@
             scores = dot(q_ref[rows, :], kt_ref[...])
             weights = jnp.exp2(scores - jnp.max(scores, axis=1, keepdims=True)).astype(BF16)
             mixed = dot(weights, v_ref[...])
-            out_ref[l, rows, :] = (mixed / mixed[:, HEAD_DIM : HEAD_DIM + 1]).astype(BF16)
+            own_ref[l, rows, :] = (mixed / mixed[:, HEAD_DIM : HEAD_DIM + 1]).astype(BF16)
             return carry
-        return lax.fori_loop(0, TOKENS // Q_ROWS, one_block, carry)
+        lax.fori_loop(0, TOKENS // Q_ROWS, one_block, 0)
+        ring(me, lambda k, peer: send_out(l, k, peer).start())
+        arrived[me, l] = own_ref[l, rows_of(me), :]
+        return carry
+
+    def rows_of(peer):
+        return pl.ds(pl.multiple_of(peer * tokens, tokens), tokens)
+
+    def send_out(l, k, peer):
+        return remote(
+            own_ref.at[l, rows_of(peer)], arrived.at[me, l], out_send.at[k, l], out_recv.at[me, l], {"seq": peer}
+        )
+
+    def wait_out(k, peer):
+        def one(l, carry):
+            remote(
+                own_ref.at[l, rows_of(peer)], arrived.at[peer, l], out_send.at[k, l], out_recv.at[peer, l], {"seq": peer}
+            ).wait()
+            return carry
+
+        lax.fori_loop(0, count, one, 0)
 
     lax.fori_loop(0, count, one_latent, 0)
-
-
-def attend(lat, patch, shift, scale, wq, wk, wv):
-    count = lat.shape[0]
+    ring(me, wait_out)
+    for l in range(count):
+        heads = [arrived[h, l].astype(F32)[:, :HEAD_DIM] for h in range(HEADS)]
+        out_ref[l * tokens : (l + 1) * tokens, :] = jnp.concatenate(heads, axis=1).astype(BF16)
+
+
+def attend(lat, cols, patch, wq, wk, wv):
+    count, channels, tokens = lat.shape
     pos = position_rows()
     centred = jnp.asarray((pos - pos.mean(axis=1, keepdims=True)).astype(np.float32))
     vmem = pl.BlockSpec(memory_space=pltpu.VMEM)
     return pl.pallas_call(
         attend_kernel,
-        out_shape=jax.ShapeDtypeStruct((count, TOKENS, LANES), BF16),
-        in_specs=[vmem] * 8,
-        out_specs=vmem,
+        out_shape=(jax.ShapeDtypeStruct((count * tokens, D), BF16), jax.ShapeDtypeStruct((8, count, D), F32)),
+        in_specs=[vmem] * 7,
+        out_specs=(vmem, vmem),
         scratch_shapes=[
+            pltpu.VMEM((HEADS, count, channels, tokens), BF16),
+            pltpu.VMEM((HEADS,) + cols.shape, F32),
+            pltpu.VMEM((HEADS, count, tokens, LANES), BF16),
+            pltpu.VMEM((count, TOKENS, LANES), BF16),
+        ]
+        + [pltpu.SemaphoreType.DMA((HEADS,))] * 4
+        + [pltpu.SemaphoreType.DMA((HEADS, count))] * 2
+        + [
             pltpu.VMEM((count, BASE, TOKENS), BF16),
             pltpu.VMEM((BASE, D), F32),
             pltpu.VMEM((count * ROWS, D), BF16),
@@ -138,8 +208,9 @@
             pltpu.VMEM((TOKENS, LANES), BF16),
             pltpu.VMEM((HEAD_DIM, TOKENS), BF16),
         ],
+        compiler_params=pltpu.CompilerParams(collective_id=1, has_side_effects=True),
         cost_estimate=pl.CostEstimate(flops=8 * 10**9, bytes_accessed=4 * 10**6, transcendentals=6 * 10**6),
-    )(lat, patch, centred, shift, scale, wq, wk, wv)
+    )(lat, cols, patch, centred, wq, wk, wv)
 
 
 def feed_forward_kernel(
@@ -239,11 +310,7 @@
     onehot = (classes[:, None] == jnp.arange(CLASSES + 1, dtype=jnp.int32)[None, :]).astype(BF16)
     conditioning = vector + dot(onehot, label_table)
     own_columns = dot(jax.nn.silu(conditioning).astype(BF16), ada_weight)
-    modulation = lax.all_gather(own_columns, "seq", axis=1, tiled=True)
-    pieces = [modulation[:, number * D : (number + 1) * D] for number in range(8)]
-
     lat_t = jnp.transpose(latents, (0, 2, 1)).astype(BF16)
-    lat_all = lax.all_gather(lat_t, "seq", axis=2, tiled=True)
     blocks = w_qkv.T.reshape(3, HEAD_DIM, D)
     got = jnp.stack(
         [
@@ -252,11 +319,8 @@
         ]
     )
     head_w = [lax.dynamic_index_in_dim(got, (HEADS * kind + place) % 3, 0, False) for kind in range(3)]
-    attended = attend(lat_all, w_patch, pieces[0], pieces[1], *head_w)
-    arrived = lax.all_to_all(
-        attended[:, :, :HEAD_DIM].reshape(count, HEADS, tok_count, HEAD_DIM), "seq", split_axis=1, concat_axis=1
-    )
-    attended = jnp.transpose(arrived, (0, 2, 1, 3)).reshape(count * tok_count, D)
+    attended, mods = attend(lat_t, own_columns, w_patch, *head_w)
+    pieces = [mods[n] for n in range(8)]
 
     pos = jnp.asarray(position_rows().astype(np.float32))
     columns = pos[:GRID]

time: 225 us -> 217 us (0.964)
  blocking collectives: 69.6 us -> 17.1 us
  Pallas kernels: 46.1 us -> 77 us
  waiting for transfers between devices: 41.3 us -> 68.3 us
  local copies, waits for them, and re-layouts: 22.4 us -> 10.9 us
  starting transfers between devices: 18.9 us -> 14.9 us
    all_gather x1, waiting for transfers between devices: 8.77 us -> 68.3 us  [shards(): lax.all_gather(jnp.concatenate([w_fc1.T, w_fc2, w_proj.T], axis=0), 'seq'...]
    all_gather x2 -> x0, blocking collectives: 52.1 us -> none  [the longest x1 31.4 us: shards(): lat_all = lax.all_gather(lat_t, 'seq', axis=2, tiled=True)]
    pallas_call x1, Pallas kernels: 24.7 us -> 59.6 us  [attend(): pl.pallas_call(attend_kernel, out_shape=(jax.ShapeDtypeStruct((count * to...]
    all_to_all x1 -> x0, waiting for transfers between devices: 32.5 us -> none  [shards(): lax.all_to_all(attended[:, :, :HEAD_DIM].reshape(count, HEADS, tok_count,...]
    all_to_all x1 -> x0, starting transfers between devices: 4.72 us -> none  [shards(): lax.all_to_all(attended[:, :, :HEAD_DIM].reshape(count, HEADS, tok_count,...]
    pallas_call x1, Pallas kernels: 21.4 us -> 17.3 us  [feed_forward(): pl.pallas_call(feed_forward_kernel, grid=(stacked.shape[0] // group,), ou...]
    transpose x1 -> x0, local copies, waits for them, and re-layouts: 3.59 us -> none  [shards(): jnp.transpose(arrived, (0, 2, 1, 3)).reshape(count * tok_count, D)]
    dot_general x1 -> x0, local copies, waits for them, and re-layouts: 3 us -> none  [dot(): lax.dot_general(a, b, dims, precision=precision, preferred_element_type=F32)]
  transfers between devices with their start and end apart: 6 -> 5, of which waited for: 2 -> 1; matrix products, arithmetic and copies ran while one was open for 10% -> 6% of each run, Pallas kernels for 11% -> 28%
where the time goes in v3:
time: 217 us; the launch traced here: 216 us
  Pallas kernels  77 us (35%)
  waiting for transfers between devices  68.3 us (31%)
  blocking collectives  17.1 us (8%)
  between operations  15 us (7%)
  starting transfers between devices  14.9 us (7%)
  local copies, waits for them, and re-layouts  10.9 us (5%)
  matrix products  7.29 us (3%)
  other arithmetic  5.61 us (3%)
    all_gather x1, waiting for transfers between devices, shards(): lax.all_gather(jnp.concatenate([w_fc1.T, w_fc2, w_proj.T], axis=0), 'seq'...  68.3 us
    pallas_call x1, Pallas kernels, attend(): pl.pallas_call(attend_kernel, out_shape=(jax.ShapeDtypeStruct((count * to...  59.6 us
    pallas_call x1, Pallas kernels, feed_forward(): pl.pallas_call(feed_forward_kernel, grid=(stacked.shape[0] // group,), ou...  17.3 us
    ppermute x3, starting transfers between devices, shards(): lax.ppermute(blocks[j], 'seq', [(s, (3 * s + j) % HEADS) for s in range(H...  11.6 us
    all_gather x1, blocking collectives, shards(): hidden_time = lax.all_gather(hidden_own, 'lat', axis=1, tiled=True)  10.2 us
    dot_general x5, matrix products, dot(): lax.dot_general(a, b, dims, precision=precision, preferred_element_type=F32)  7.29 us
    unnamed x1, blocking collectives  6.9 us
  transfers between devices with their start and end apart: 5, of which 1 were waited for; matrix products, arithmetic and copies ran while one was open for 6% of the time, Pallas kernels for 28%

profile of v3, /device:TPU:1, one launch (start us, length us, event | category | flops | bytes accessed | tf_op | source)
XLA Modules:
  0.0 216.1 jit_solution(4935679854038854469)
XLA Ops:
  6.5 2.8 %pad_maximum_fusion = bf16[648,1152]{1,0:T(8,128)(2,1)} fusion(bf16[72,1152]{1,0:T(8,128)(2,1)} %bitcast.63, bf16[288,1152]{1,0:T(8,128)(2,1)} %param.32, bf16[288,1152]{1,0:T(8,128)(2,1)} %bitcast.60), kind=kLoop, calls=%fused_computation.4 | loop fusion | flops 4478976 | bytes 2985984 | tf_op jit(solution)/shard_map/concatenate | solution.py:300
  9.5 0.9 fusion.19
  10.3 5.6 %collective-permute-start.2 = (bf16[72,1152]{1,0:T(8,128)(2,1)}, bf16[72,1152]{1,0:T(8,128)(2,1)S(1)}, u32[]{:S(2)}, u32[]{:S(2)}) collective-permute-start(bf16[72,1152]{1,0:T(8,128)(2,1)} %get-tuple-element.13), channel_id=1, source_target_pairs={{0,2},{1,5},{2,8},{3,11},{4,14},{5,1},{6,4},{7,7},{8,10},{9,13},{1... | collective-permute-start | bytes 497672 | tf_op jit(solution)/shard_map/ppermute | solution.py:317
  16.0 1.6 collective-permute-start
  17.5 4.4 %collective-permute-start.1 = (bf16[72,1152]{1,0:T(8,128)(2,1)}, bf16[72,1152]{1,0:T(8,128)(2,1)}, u32[]{:S(2)}, u32[]{:S(2)}) collective-permute-start(bf16[72,1152]{1,0:T(8,128)(2,1)} %get-tuple-element.14), channel_id=1, source_target_pairs={{0,1},{1,4},{2,7},{3,10},{4,13},{5,0},{6,3},{7,6},{8,9},{9,12},{10... | collective-permute-start | bytes 497672 | tf_op jit(solution)/shard_map/ppermute | solution.py:317
  21.9 0.6 dynamic-slice
  23.2 0.2 dynamic-update-slice
  23.5 6.9 %all-reduce = s32[24]{0:T(128)S(1)} all-reduce(s32[24]{0:T(128)S(1)} %dynamic-update-slice), channel_id=1, replica_groups=mesh['cfg'=2,'lat'=4,'seq'=16] {'lat'}, use_global_device_ids=true, to_apply=%add | all-reduce | flops 24 | bytes 192
  30.4 0.1 fusion.8
  30.5 1.1 fusion.5
  31.6 10.2 %all-gather.1 = bf16[4,288,24]{1,2,0:T(8,128)(2,1)S(1)} all-gather(bf16[1,288,24]{1,2,0:T(8,128)(2,1)S(1)} %fusion.5), channel_id=1, replica_groups=mesh['cfg'=2,'lat'=4,'seq'=16] {'lat'}, dimensions={0}, use_global_device_ids=true | all-gather | bytes 69120 | tf_op jit(solution)/shard_map/all_gather | solution.py:307
  41.9 0.1 reshape.58
  42.0 0.3 fusion.20
  42.3 0.7 all_to_all.14
  43.0 3.3 %all-to-all-start = ((f32[4,6,288]{2,1,0:T(8,128)}), f32[4,6,288]{2,1,0:T(8,128)S(1)}, u32[]{:S(2)}, u32[]{:S(2)}) async-start(f32[4,6,288]{2,1,0:T(8,128)} %all_to_all.14), calls=%async_computation | async-start | bytes 98304 | tf_op jit(solution)/shard_map/all_to_all | solution.py:309
  46.3 0.8 constant_dynamic-slice_fusion
  47.1 0.6 convert_bitcast_fusion.lat_ref
  47.7 0.9 broadcast_add_fusion
  48.7 1.7 copy.30.out_w_ref
  51.0 0.1 all_to_all.17
  51.1 2.7 %fusion.2.cols_ref = f32[6,576]{1,0:T(8,128)} fusion(bf16[1152,576]{0,1:T(8,128)(2,1)} %param.28, f32[6,1152]{1,0:T(8,128)S(1)} %all_to_all.17, bf16[1001,1152]{1,0:T(8,128)(2,1)S(1)} %copy-done, s32[6]{0:T(128)S(1)} %broadcast_select_fusion), kind=kOutput, calls=%fused_computation.18 | convolution fusion | flops 21847926 | bytes 3674904 | tf_op jit(solution)/shard_map/dot_general | solution.py:42
  53.9 1.0 pad_maximum_fusion.1
  54.9 0.8 dynamic-slice_bitcast_fusion
  55.7 59.6 %shard_map.172 = (bf16[384,1152]{1,0:T(8,128)(2,1)}, f32[8,6,1152]{2,1,0:T(8,128)}) custom-call(bf16[6,16,64]{2,1,0:T(8,128)(2,1)} %convert_bitcast_fusion.lat_ref, f32[6,576]{1,0:T(8,128)} %fusion.2.cols_ref, bf16[16,1152]{1,0:T(8,128)(2,1)} %patch_ref.1, f32[64,1152]{1,0:T(8,128)} %constant.60.clone.pos_ref, bf16[72,1152]{1,0:T(8,128)(2,1)} %get-tuple-element.11.wq_ref, ...), custom_call_target="tpu_custom_call" | custom-call | flops 8000000000 | bytes 4000000 | tf_op jit(solution)/shard_map/pallas_call | solution.py:185
  115.3 1.6 slice_bitcast_fusion
  116.9 68.3 %all-gather.4.cloned.1.call-done = bf16[10368,1152]{1,0:T(8,128)(2,1)} async-done(((bf16[648,1152]{1,0:T(8,128)(2,1)}), bf16[10368,1152]{1,0:T(8,128)(2,1)}) %all-gather.4.cloned.1.call-update) | async-done | bytes 23887888 | tf_op jit(solution)/shard_map/all_gather | solution.py:300
  185.2 2.0 slice.50
  187.2 1.5 convolution_multiply_fusion
  188.7 1.7 fusion
  190.4 17.3 %shard_map.173 = f32[8,384]{1,0:T(8,128)} custom-call(f32[1]{0:T(128)S(6)} %copy.37.guidance_ref, f32[384,1152]{1,0:T(8,128)} %bitcast.57, f32[6,1152]{1,0:T(8,128)} %get-tuple-element.19.shift_ref, f32[6,1152]{1,0:T(8,128)} %get-tuple-element.18.scale_ref, f32[6,1152]{1,0:T(8,128)} %get-tuple-element.17.gate_ref, ...), custom_call_target="tpu_custom_call" | custom-call | flops 8000000000 | bytes 24000000 | tf_op jit(solution)/shard_map/pallas_call | solution.py:273
  207.8 0.8 reshape.52
  208.6 0.6 copy.31
  (36 shorter events, 0.2 us)
Async XLA Ops:
  6.5 44.6 %copy-start = (bf16[1001,1152]{1,0:T(8,128)(2,1)S(1)}, bf16[1001,1152]{1,0:T(8,128)(2,1)}, u32[]{:S(2)}) copy-start(bf16[1001,1152]{1,0:T(8,128)(2,1)} %param.25) | copy-start | bytes 6918916
  6.5 178.6 %all-gather.4.cloned.1.call-start = ((), (), s32[]{:S(2)}) async-start(), calls=%async_computation.1 | async-start | bytes 25380864 | tf_op jit(solution)/shard_map/all_gather | solution.py:300
  6.5 2.9 %copy-start.2 = (bf16[1152,216]{0,1:T(8,128)(2,1)S(1)}, bf16[1152,216]{0,1:T(8,128)(2,1)}, u32[]{:S(2)}) copy-start(bf16[1152,216]{0,1:T(8,128)(2,1)} %param.29) | copy-start | bytes 1492996
  9.4 12.6 %copy-start.10 = (u32[128]{0:T(128)S(1)}, u32[128]{0:T(128)}, u32[]{:S(2)}) copy-start(u32[128]{0:T(128)} %constant.72) | copy-start | bytes 1540
  9.4 13.8 %copy-start.7 = (s32[6]{0:T(128)S(1)}, s32[6]{0:T(128)}, u32[]{:S(2)}) copy-start(s32[6]{0:T(128)} %param.19) | copy-start | bytes 76
  9.4 32.6 %copy-start.1 = (bf16[1152,288]{0,1:T(8,128)(2,1)S(1)}, bf16[1152,288]{0,1:T(8,128)(2,1)}, u32[]{:S(2)}) copy-start(bf16[1152,288]{0,1:T(8,128)(2,1)} %param.27) | copy-start | bytes 1990660
  9.4 36.8 %copy-start.8 = (s32[6]{0:T(128)S(1)}, s32[6]{0:T(128)}, u32[]{:S(2)}) copy-start(s32[6]{0:T(128)} %param.20) | copy-start | bytes 76
  9.4 37.6 %copy-start.3 = (f32[6,64,16]{1,2,0:T(8,128)S(1)}, f32[6,64,16]{1,2,0:T(8,128)}, u32[]{:S(2)}) copy-start(f32[6,64,16]{1,2,0:T(8,128)} %param.18) | copy-start | bytes 73732
  10.3 43.6 %collective-permute-start.2 = (bf16[72,1152]{1,0:T(8,128)(2,1)}, bf16[72,1152]{1,0:T(8,128)(2,1)S(1)}, u32[]{:S(2)}, u32[]{:S(2)}) collective-permute-start(bf16[72,1152]{1,0:T(8,128)(2,1)} %get-tuple-element.13), channel_id=1, source_target_pairs={{0,2},{1,5},{2,8},{3,11},{4,14},{5,1},{6,4},{7,7},{8,10},{9,13},{1... | collective-permute-start | bytes 497672 | tf_op jit(solution)/shard_map/ppermute | solution.py:317
  16.0 37.9 %collective-permute-start = (bf16[72,1152]{1,0:T(8,128)(2,1)}, bf16[72,1152]{1,0:T(8,128)(2,1)S(1)}, u32[]{:S(2)}, u32[]{:S(2)}) collective-permute-start(bf16[72,1152]{1,0:T(8,128)(2,1)} %get-tuple-element.12), channel_id=1, source_target_pairs={{0,0},{1,3},{2,6},{3,9},{4,12},{5,15},{6,2},{7,5},{8,8},{9,11},{10... | collective-permute-start | bytes 497672 | tf_op jit(solution)/shard_map/ppermute | solution.py:317
  17.5 36.3 %collective-permute-start.1 = (bf16[72,1152]{1,0:T(8,128)(2,1)}, bf16[72,1152]{1,0:T(8,128)(2,1)}, u32[]{:S(2)}, u32[]{:S(2)}) collective-permute-start(bf16[72,1152]{1,0:T(8,128)(2,1)} %get-tuple-element.14), channel_id=1, source_target_pairs={{0,1},{1,4},{2,7},{3,10},{4,13},{5,0},{6,3},{7,6},{8,9},{9,12},{10... | collective-permute-start | bytes 497672 | tf_op jit(solution)/shard_map/ppermute | solution.py:317
  43.0 8.1 %all-to-all-start = ((f32[4,6,288]{2,1,0:T(8,128)}), f32[4,6,288]{2,1,0:T(8,128)S(1)}, u32[]{:S(2)}, u32[]{:S(2)}) async-start(f32[4,6,288]{2,1,0:T(8,128)} %all_to_all.14), calls=%async_computation | async-start | bytes 98304 | tf_op jit(solution)/shard_map/all_to_all | solution.py:309
  185.2 2.0 copy-start.9
  187.2 1.5 copy-start.4
  190.4 18.1 %copy-start.5 = (f32[6]{0:T(128)S(1)}, f32[6]{0:T(128)}, u32[]{:S(2)}) copy-start(f32[6]{0:T(128)} %param.23) | copy-start | bytes 76
  190.4 18.1 %copy-start.6 = (f32[6]{0:T(128)S(1)}, f32[6]{0:T(128)}, u32[]{:S(2)}) copy-start(f32[6]{0:T(128)} %param.22) | copy-start | bytes 76
Sparse Core Ops, SparseCore 0:
  9.6 175.5 all-gather.3

commit v4 on v3

--- a/solution.py
+++ b/solution.py
@@ -214,79 +214,95 @@
 
 
 def feed_forward_kernel(
-    guidance_ref, state_ref, shift_ref, scale_ref, gate_ref, last_shift_ref, last_scale_ref, fc1_ref, fc2_ref, out_w_ref,
-    out_ref, normed_ref, total_ref, noise_ref, partner_ref, send_sem, recv_sem,
+    guidance_ref, state_ref, mods_ref, stacked_ref, out_w_ref,
+    out_ref, fc1_ref, fc2_ref, normed_ref, theirs_ref, part_ref, got_ref, total_ref, noise_ref, partner_ref,
+    load_sem, send_sem, recv_sem,
 ):
-    step = pl.program_id(0)
     side = lax.axis_index("cfg")
-    count = shift_ref.shape[0]
+    peer = {"cfg": 1 - side}
+    count = mods_ref.shape[1]
     tokens = state_ref.shape[0] // count
+    units = fc1_ref.shape[1]
     barrier = pltpu.get_barrier_semaphore()
-
-    @pl.when(step == 0)
-    def _():
-        pl.semaphore_signal(barrier, inc=1, device_id={"cfg": 1 - side}, device_id_type=MESH)
-        for l in range(count):
-            rows = slice(l * tokens, (l + 1) * tokens)
-            normed_ref[rows, :] = (
-                layer_norm(state_ref[rows, :]) * (1.0 + scale_ref[l : l + 1, :]) + shift_ref[l : l + 1, :]
-            ).astype(BF16)
-        total_ref[...] = jnp.zeros_like(total_ref)
-
-    units = fc1_ref.shape[0] * fc1_ref.shape[1]
-    hidden = dot(normed_ref[...], fc1_ref[...].reshape(units, D), NT)
-    hidden = jax.nn.gelu(hidden, approximate=True).astype(BF16)
-    total_ref[...] += dot(hidden, fc2_ref[...].reshape(units, D))
-
-    @pl.when(step == pl.num_programs(0) - 1)
-    def _():
-        for l in range(count):
-            rows = slice(l * tokens, (l + 1) * tokens)
-            state = state_ref[rows, :] + gate_ref[l : l + 1, :] * total_ref[rows, :]
-            normed_ref[rows, :] = (
-                layer_norm(state) * (1.0 + last_scale_ref[l : l + 1, :]) + last_shift_ref[l : l + 1, :]
-            ).astype(BF16)
-        noise_ref[...] = dot(out_w_ref[...], normed_ref[...], (((0,), (1,)), ((), ())))
-        pl.semaphore_wait(barrier, 1)
-        copy = pltpu.make_async_remote_copy(
-            src_ref=noise_ref.at[pl.ds(pl.multiple_of((1 - side) * 8, 8), 8)],
-            dst_ref=partner_ref,
-            send_sem=send_sem,
-            recv_sem=recv_sem,
-            device_id={"cfg": 1 - side},
-            device_id_type=MESH,
-        )
-        copy.start()
-        copy.wait()
-        own = noise_ref[pl.ds(pl.multiple_of(side * 8, 8), 8), :]
-        cond_noise = jnp.where(side == 0, own, partner_ref[...])
-        free_noise = jnp.where(side == 0, partner_ref[...], own)
-        out_ref[...] = free_noise + guidance_ref[0] * (cond_noise - free_noise)
-
-
-def feed_forward(state, pieces, stacked, w_out, guidance, rows):
+    pl.semaphore_signal(barrier, inc=1, device_id=peer, device_id_type=MESH)
+    loads = [
+        pltpu.make_async_copy(stacked_ref.at[:, n * units : (n + 1) * units, :], target, load_sem.at[n])
+        for n, target in enumerate((fc1_ref, fc2_ref))
+    ]
+    for load in loads:
+        load.start()
+    for l in range(count):
+        rows = slice(l * tokens, (l + 1) * tokens)
+        normed_ref[rows, :] = (
+            layer_norm(state_ref[rows, :]) * (1.0 + mods_ref[4, l : l + 1, :]) + mods_ref[3, l : l + 1, :]
+        ).astype(BF16)
+    pl.semaphore_wait(barrier, 1)
+    hand = remote(normed_ref, theirs_ref, send_sem.at[0], recv_sem.at[0], peer)
+    hand.start()
+
+    def half_of(source_ref, target_ref):
+        target_ref[...] = jnp.zeros_like(target_ref)
+
+        def one(g, carry):
+            group = pl.ds(pl.multiple_of(g * 8, 8), 8)
+            hidden = dot(source_ref[...], fc1_ref[group].reshape(8 * units, D), NT)
+            hidden = jax.nn.gelu(hidden, approximate=True).astype(BF16)
+            target_ref[...] += dot(hidden, fc2_ref[group].reshape(8 * units, D))
+            return carry
+
+        lax.fori_loop(0, HEADS // 8, one, 0)
+
+    for load in loads:
+        load.wait()
+    hand.wait()
+    half_of(theirs_ref, part_ref)
+    back = remote(part_ref, got_ref, send_sem.at[1], recv_sem.at[1], peer)
+    back.start()
+    half_of(normed_ref, total_ref)
+    back.wait()
+    for l in range(count):
+        rows = slice(l * tokens, (l + 1) * tokens)
+        state = state_ref[rows, :] + mods_ref[5, l : l + 1, :] * (total_ref[rows, :] + got_ref[rows, :])
+        normed_ref[rows, :] = (
+            layer_norm(state) * (1.0 + mods_ref[7, l : l + 1, :]) + mods_ref[6, l : l + 1, :]
+        ).astype(BF16)
+    noise_ref[...] = dot(out_w_ref[...], normed_ref[...], (((0,), (1,)), ((), ())))
+    last = remote(
+        noise_ref.at[pl.ds(pl.multiple_of((1 - side) * 8, 8), 8)], partner_ref, send_sem.at[2], recv_sem.at[2], peer
+    )
+    last.start()
+    last.wait()
+    own = noise_ref[pl.ds(pl.multiple_of(side * 8, 8), 8), :]
+    cond_noise = jnp.where(side == 0, own, partner_ref[...])
+    free_noise = jnp.where(side == 0, partner_ref[...], own)
+    out_ref[...] = free_noise + guidance_ref[0] * (cond_noise - free_noise)
+
+
+def feed_forward(state, mods, stacked, w_out, guidance, units):
     tokens = state.shape[0]
-    shift, scale, gate, last_shift, last_scale = pieces
     whole = pl.BlockSpec(memory_space=pltpu.VMEM)
-    group = 4
-    weights = [pl.BlockSpec((group, rows, D), lambda i, b=b: (i, b, 0)) for b in range(2)]
     return pl.pallas_call(
         feed_forward_kernel,
-        grid=(stacked.shape[0] // group,),
         out_shape=jax.ShapeDtypeStruct((8, tokens), F32),
-        in_specs=[pl.BlockSpec(memory_space=pltpu.SMEM)] + [whole] * 6 + weights + [whole],
+        in_specs=[pl.BlockSpec(memory_space=pltpu.SMEM), whole, whole, pl.BlockSpec(memory_space=pl.ANY), whole],
         out_specs=whole,
         scratch_shapes=[
+            pltpu.VMEM((HEADS, units, D), BF16),
+            pltpu.VMEM((HEADS, units, D), BF16),
             pltpu.VMEM((tokens, D), BF16),
+            pltpu.VMEM((tokens, D), BF16),
+            pltpu.VMEM((tokens, D), F32),
+            pltpu.VMEM((tokens, D), F32),
             pltpu.VMEM((tokens, D), F32),
             pltpu.VMEM((16, tokens), F32),
             pltpu.VMEM((8, tokens), F32),
-            pltpu.SemaphoreType.DMA,
-            pltpu.SemaphoreType.DMA,
+            pltpu.SemaphoreType.DMA((2,)),
+            pltpu.SemaphoreType.DMA((3,)),
+            pltpu.SemaphoreType.DMA((3,)),
         ],
         compiler_params=pltpu.CompilerParams(collective_id=0, has_side_effects=True),
-        cost_estimate=pl.CostEstimate(flops=8 * 10**9, bytes_accessed=24 * 10**6, transcendentals=2 * 10**6),
-    )(guidance, state, shift, scale, gate, last_shift, last_scale, stacked, stacked, w_out)
+        cost_estimate=pl.CostEstimate(flops=8 * 10**9, bytes_accessed=12 * 10**6, transcendentals=2 * 10**6),
+    )(guidance, state, mods, stacked, w_out)
 
 
 def shards(
@@ -296,9 +312,11 @@
     count, tok_count, channels = latents.shape
     side = lax.axis_index("cfg")
     place = lax.axis_index("seq")
-    rows = w_fc2.shape[0]
-    stacked = lax.all_gather(jnp.concatenate([w_fc1.T, w_fc2, w_proj.T], axis=0), "seq", axis=0)
-    proj_full = stacked[:, 2 * rows :].reshape(D, D)
+    half = w_fc2.shape[0] // 2
+    fc1_half = lax.dynamic_slice_in_dim(w_fc1.T, side * half, half, 0)
+    fc2_half = lax.dynamic_slice_in_dim(w_fc2, side * half, half, 0)
+    stacked = lax.all_gather(jnp.concatenate([fc1_half, fc2_half, w_proj.T], axis=0), "seq", axis=0)
+    proj_full = stacked[:, 2 * half :].reshape(D, D)
 
     classes = jnp.where(side == 0, labels, CLASSES)
     steps_all = lax.all_gather(timesteps, "lat", axis=0, tiled=True)
@@ -320,7 +338,6 @@
     )
     head_w = [lax.dynamic_index_in_dim(got, (HEADS * kind + place) % 3, 0, False) for kind in range(3)]
     attended, mods = attend(lat_t, own_columns, w_patch, *head_w)
-    pieces = [mods[n] for n in range(8)]
 
     pos = jnp.asarray(position_rows().astype(np.float32))
     columns = pos[:GRID]
@@ -328,8 +345,8 @@
     own_pos = (columns[None] + lines[:, None]).reshape(tok_count, D)
     state = dot(latents.reshape(-1, channels).astype(BF16), w_patch).reshape(count, tok_count, D) + own_pos[None]
     projected = dot(attended, proj_full, NT).reshape(count, tok_count, D)
-    state = state + pieces[2][:, None, :] * projected
-    guided = feed_forward(state.reshape(-1, D), pieces[3:], stacked, w_out, guidance, rows)
+    state = state + mods[2][:, None, :] * projected
+    guided = feed_forward(state.reshape(-1, D), mods, stacked, w_out, guidance, half)
     half_width = channels // 2
     own_latent = lax.dynamic_slice_in_dim(latents, side * half_width, half_width, 2)
     guided = guided.T.reshape(count, tok_count, half_width)

time: 217 us -> 169 us (0.78)
  waiting for transfers between devices: 68.3 us -> 11.7 us
  Pallas kernels: 77 us -> 85.9 us
    all_gather x1, waiting for transfers between devices: 68.3 us -> 11.4 us  [shards(): lax.all_gather(jnp.concatenate([fc1_half, fc2_half, w_proj.T], axis=0), '...]
    pallas_call x1, Pallas kernels: 59.6 us -> 65.9 us  [attend(): pl.pallas_call(attend_kernel, out_shape=(jax.ShapeDtypeStruct((count * to...]
    pallas_call x1, Pallas kernels: 17.3 us -> 20 us  [feed_forward(): pl.pallas_call(feed_forward_kernel, out_shape=jax.ShapeDtypeStruct((8, to...]
  transfers between devices with their start and end apart: 5 -> 5, of which waited for: 1 -> 2; matrix products, arithmetic and copies ran while one was open for 6% -> 7% of each run, Pallas kernels for 28% -> 39%
where the time goes in v4:
time: 169 us; the launch traced here: 168 us
  Pallas kernels  85.9 us (51%)
  blocking collectives  17 us (10%)
  starting transfers between devices  15 us (9%)
  between operations  15 us (9%)
  waiting for transfers between devices  11.7 us (7%)
  local copies, waits for them, and re-layouts  11.5 us (7%)
  matrix products  7.22 us (4%)
  other arithmetic  4.71 us (3%)
    pallas_call x1, Pallas kernels, attend(): pl.pallas_call(attend_kernel, out_shape=(jax.ShapeDtypeStruct((count * to...  65.9 us
    pallas_call x1, Pallas kernels, feed_forward(): pl.pallas_call(feed_forward_kernel, out_shape=jax.ShapeDtypeStruct((8, to...  20 us
    ppermute x3, starting transfers between devices, shards(): lax.ppermute(blocks[j], 'seq', [(s, (3 * s + j) % HEADS) for s in range(H...  11.7 us
    all_gather x1, waiting for transfers between devices, shards(): lax.all_gather(jnp.concatenate([fc1_half, fc2_half, w_proj.T], axis=0), '...  11.4 us
    all_gather x1, blocking collectives, shards(): hidden_time = lax.all_gather(hidden_own, 'lat', axis=1, tiled=True)  9.69 us
    unnamed x1, blocking collectives  7.32 us
    dot_general x5, matrix products, dot(): lax.dot_general(a, b, dims, precision=precision, preferred_element_type=F32)  7.22 us
  transfers between devices with their start and end apart: 5, of which 2 were waited for; matrix products, arithmetic and copies ran while one was open for 7% of the time, Pallas kernels for 39%

profile of v4, /device:TPU:1, one launch (start us, length us, event | category | flops | bytes accessed | tf_op | source)
XLA Modules:
  0.0 168.2 jit_solution(7455690638408980082)
XLA Ops:
  6.5 1.2 constant_dynamic-slice_fusion
  7.7 1.0 dynamic-slice_bitcast_fusion
  8.7 2.0 %pad_maximum_fusion = bf16[360,1152]{1,0:T(8,128)(2,1)} fusion(bf16[72,1152]{1,0:T(8,128)(2,1)} %bitcast.52, bf16[144,1152]{1,0:T(8,128)(2,1)S(1)} %constant_dynamic-slice_fusion, bf16[144,1152]{1,0:T(8,128)(2,1)S(1)} %dynamic-slice_bitcast_fusion), kind=kLoop, calls=%fused_computation.4 | loop fusion | flops 2488320 | bytes 1658880 | tf_op jit(solution)/shard_map/concatenate | solution.py:318
  10.7 0.8 fusion.19
  11.6 5.8 %collective-permute-start.2 = (bf16[72,1152]{1,0:T(8,128)(2,1)}, bf16[72,1152]{1,0:T(8,128)(2,1)S(1)}, u32[]{:S(2)}, u32[]{:S(2)}) collective-permute-start(bf16[72,1152]{1,0:T(8,128)(2,1)} %get-tuple-element.13), channel_id=1, source_target_pairs={{0,2},{1,5},{2,8},{3,11},{4,14},{5,1},{6,4},{7,7},{8,10},{9,13},{1... | collective-permute-start | bytes 497672 | tf_op jit(solution)/shard_map/ppermute | solution.py:335
  17.3 1.6 collective-permute-start
  18.9 4.4 %collective-permute-start.1 = (bf16[72,1152]{1,0:T(8,128)(2,1)}, bf16[72,1152]{1,0:T(8,128)(2,1)}, u32[]{:S(2)}, u32[]{:S(2)}) collective-permute-start(bf16[72,1152]{1,0:T(8,128)(2,1)} %get-tuple-element.14), channel_id=1, source_target_pairs={{0,1},{1,4},{2,7},{3,10},{4,13},{5,0},{6,3},{7,6},{8,9},{9,12},{10... | collective-permute-start | bytes 497672 | tf_op jit(solution)/shard_map/ppermute | solution.py:335
  23.3 0.6 dynamic-slice.4
  24.6 0.2 dynamic-update-slice
  24.8 7.3 %all-reduce = s32[24]{0:T(128)S(1)} all-reduce(s32[24]{0:T(128)S(1)} %dynamic-update-slice), channel_id=1, replica_groups=mesh['cfg'=2,'lat'=4,'seq'=16] {'lat'}, use_global_device_ids=true, to_apply=%add | all-reduce | flops 24 | bytes 192
  32.3 1.1 fusion.5
  33.4 9.7 %all-gather.1 = bf16[4,288,24]{1,2,0:T(8,128)(2,1)S(1)} all-gather(bf16[1,288,24]{1,2,0:T(8,128)(2,1)S(1)} %fusion.5), channel_id=1, replica_groups=mesh['cfg'=2,'lat'=4,'seq'=16] {'lat'}, dimensions={0}, use_global_device_ids=true | all-gather | bytes 69120 | tf_op jit(solution)/shard_map/all_gather | solution.py:325
  43.3 0.3 fusion.20
  43.6 0.7 all_to_all.14
  44.2 3.3 %all-to-all-start = ((f32[4,6,288]{2,1,0:T(8,128)}), f32[4,6,288]{2,1,0:T(8,128)S(1)}, u32[]{:S(2)}, u32[]{:S(2)}) async-start(f32[4,6,288]{2,1,0:T(8,128)} %all_to_all.14), calls=%async_computation | async-start | bytes 98304 | tf_op jit(solution)/shard_map/all_to_all | solution.py:327
  47.5 0.8 constant_dynamic-slice_fusion.1
  48.3 0.6 convert_bitcast_fusion.lat_ref
  48.9 0.9 broadcast_add_fusion
  50.0 0.9 copy.30.out_w_ref
  51.5 0.3 all-to-all-done
  52.0 2.7 %fusion.2.cols_ref = f32[6,576]{1,0:T(8,128)} fusion(bf16[1152,576]{0,1:T(8,128)(2,1)} %param.28, f32[6,1152]{1,0:T(8,128)S(1)} %all_to_all.17, bf16[1001,1152]{1,0:T(8,128)(2,1)S(1)} %copy-done, s32[6]{0:T(128)S(1)} %broadcast_select_fusion), kind=kOutput, calls=%fused_computation.14 | convolution fusion | flops 21847926 | bytes 3674904 | tf_op jit(solution)/shard_map/dot_general | solution.py:42
  54.7 1.0 pad_maximum_fusion.1
  55.7 0.8 dynamic-slice_bitcast_fusion.1
  56.6 65.9 %shard_map.172 = (bf16[384,1152]{1,0:T(8,128)(2,1)}, f32[8,6,1152]{2,1,0:T(8,128)}) custom-call(bf16[6,16,64]{2,1,0:T(8,128)(2,1)} %convert_bitcast_fusion.lat_ref, f32[6,576]{1,0:T(8,128)} %fusion.2.cols_ref, bf16[16,1152]{1,0:T(8,128)(2,1)} %patch_ref.1, f32[64,1152]{1,0:T(8,128)} %constant.64.clone.pos_ref, bf16[72,1152]{1,0:T(8,128)(2,1)} %get-tuple-element.11.wq_ref, ...), custom_call_target="tpu_custom_call" | custom-call | flops 8000000000 | bytes 4000000 | tf_op jit(solution)/shard_map/pallas_call | solution.py:185
  122.5 0.8 slice_bitcast_fusion
  123.3 11.4 %all-gather.4.cloned.1.call-done = bf16[5760,1152]{1,0:T(8,128)(2,1)} async-done(((bf16[360,1152]{1,0:T(8,128)(2,1)}), bf16[5760,1152]{1,0:T(8,128)(2,1)}) %all-gather.4.cloned.1.call-update) | async-done | bytes 13271056 | tf_op jit(solution)/shard_map/all_gather | solution.py:318
  134.7 2.0 %slice.30 = bf16[16,72,1152]{2,1,0:T(8,128)(2,1)S(1)} slice(bf16[16,360,1152]{2,1,0:T(8,128)(2,1)} %bitcast.48), slice={[0:16], [288:360], [0:1152]} | slice | bytes 5308416 | tf_op jit(solution)/shard_map/slice | solution.py:319
  136.7 1.4 convolution_multiply_fusion
  138.2 1.6 fusion
  139.8 20.0 %shard_map.173 = f32[8,384]{1,0:T(8,128)} custom-call(f32[1]{0:T(128)S(6)} %copy.37.guidance_ref, f32[384,1152]{1,0:T(8,128)} %bitcast.46, f32[8,6,1152]{2,1,0:T(8,128)} %get-tuple-element.7.mods_ref, bf16[16,360,1152]{2,1,0:T(8,128)(2,1)} %bitcast.49, bf16[1152,16]{1,0:T(8,128)(2,1)} %copy.30.out_w_ref), custom_call_target="tpu_custom_call" | custom-call | flops 8000000000 | bytes 12000000 | tf_op jit(solution)/shard_map/pallas_call | solution.py:284
  159.8 0.8 reshape.52
  160.7 0.6 copy.31
  (40 shorter events, 0.6 us)
Async XLA Ops:
  6.5 45.4 %copy-start = (bf16[1001,1152]{1,0:T(8,128)(2,1)S(1)}, bf16[1001,1152]{1,0:T(8,128)(2,1)}, u32[]{:S(2)}) copy-start(bf16[1001,1152]{1,0:T(8,128)(2,1)} %param.25) | copy-start | bytes 6918916
  6.5 128.1 %all-gather.4.cloned.1.call-start = ((), (), s32[]{:S(2)}) async-start(), calls=%async_computation.1 | async-start | bytes 14100480 | tf_op jit(solution)/shard_map/all_gather | solution.py:318
  6.5 4.2 %copy-start.2 = (bf16[1152,216]{0,1:T(8,128)(2,1)S(1)}, bf16[1152,216]{0,1:T(8,128)(2,1)}, u32[]{:S(2)}) copy-start(bf16[1152,216]{0,1:T(8,128)(2,1)} %param.29) | copy-start | bytes 1492996
  8.7 14.6 %copy-start.11 = (u32[128]{0:T(128)S(1)}, u32[128]{0:T(128)}, u32[]{:S(2)}) copy-start(u32[128]{0:T(128)} %constant.76) | copy-start | bytes 1540
  8.7 15.8 %copy-start.8 = (s32[6]{0:T(128)S(1)}, s32[6]{0:T(128)}, u32[]{:S(2)}) copy-start(s32[6]{0:T(128)} %param.19) | copy-start | bytes 76
  8.7 34.5 %copy-start.1 = (bf16[1152,288]{0,1:T(8,128)(2,1)S(1)}, bf16[1152,288]{0,1:T(8,128)(2,1)}, u32[]{:S(2)}) copy-start(bf16[1152,288]{0,1:T(8,128)(2,1)} %param.27) | copy-start | bytes 1990660
  10.7 36.8 %copy-start.9 = (s32[6]{0:T(128)S(1)}, s32[6]{0:T(128)}, u32[]{:S(2)}) copy-start(s32[6]{0:T(128)} %param.20) | copy-start | bytes 76
  10.7 37.6 %copy-start.3 = (f32[6,64,16]{1,2,0:T(8,128)S(1)}, f32[6,64,16]{1,2,0:T(8,128)}, u32[]{:S(2)}) copy-start(f32[6,64,16]{1,2,0:T(8,128)} %param.18) | copy-start | bytes 73732
  11.6 38.4 %copy-start.5 = (bf16[1152,16]{0,1:T(8,128)(2,1)S(1)}, bf16[1152,16]{0,1:T(8,128)(2,1)}, u32[]{:S(2)}) copy-start(bf16[1152,16]{0,1:T(8,128)(2,1)} %param.33) | copy-start | bytes 110596
  11.6 43.2 %collective-permute-start.2 = (bf16[72,1152]{1,0:T(8,128)(2,1)}, bf16[72,1152]{1,0:T(8,128)(2,1)S(1)}, u32[]{:S(2)}, u32[]{:S(2)}) collective-permute-start(bf16[72,1152]{1,0:T(8,128)(2,1)} %get-tuple-element.13), channel_id=1, source_target_pairs={{0,2},{1,5},{2,8},{3,11},{4,14},{5,1},{6,4},{7,7},{8,10},{9,13},{1... | collective-permute-start | bytes 497672 | tf_op jit(solution)/shard_map/ppermute | solution.py:335
  17.3 37.4 %collective-permute-start = (bf16[72,1152]{1,0:T(8,128)(2,1)}, bf16[72,1152]{1,0:T(8,128)(2,1)S(1)}, u32[]{:S(2)}, u32[]{:S(2)}) collective-permute-start(bf16[72,1152]{1,0:T(8,128)(2,1)} %get-tuple-element.12), channel_id=1, source_target_pairs={{0,0},{1,3},{2,6},{3,9},{4,12},{5,15},{6,2},{7,5},{8,8},{9,11},{10... | collective-permute-start | bytes 497672 | tf_op jit(solution)/shard_map/ppermute | solution.py:335
  18.9 35.8 %collective-permute-start.1 = (bf16[72,1152]{1,0:T(8,128)(2,1)}, bf16[72,1152]{1,0:T(8,128)(2,1)}, u32[]{:S(2)}, u32[]{:S(2)}) collective-permute-start(bf16[72,1152]{1,0:T(8,128)(2,1)} %get-tuple-element.14), channel_id=1, source_target_pairs={{0,1},{1,4},{2,7},{3,10},{4,13},{5,0},{6,3},{7,6},{8,9},{9,12},{10... | collective-permute-start | bytes 497672 | tf_op jit(solution)/shard_map/ppermute | solution.py:335
  44.2 7.6 %all-to-all-start = ((f32[4,6,288]{2,1,0:T(8,128)}), f32[4,6,288]{2,1,0:T(8,128)S(1)}, u32[]{:S(2)}, u32[]{:S(2)}) async-start(f32[4,6,288]{2,1,0:T(8,128)} %all_to_all.14), calls=%async_computation | async-start | bytes 98304 | tf_op jit(solution)/shard_map/all_to_all | solution.py:327
  134.7 2.0 %copy-start.10 = (bf16[384,1152]{1,0:T(8,128)(2,1)S(1)}, bf16[384,1152]{1,0:T(8,128)(2,1)}, u32[]{:S(2)}) copy-start(bf16[384,1152]{1,0:T(8,128)(2,1)} %get-tuple-element.8) | copy-start | bytes 2654212
  136.7 1.5 copy-start.4
  139.8 20.8 %copy-start.6 = (f32[6]{0:T(128)S(1)}, f32[6]{0:T(128)}, u32[]{:S(2)}) copy-start(f32[6]{0:T(128)} %param.23) | copy-start | bytes 76
  139.8 20.8 %copy-start.7 = (f32[6]{0:T(128)S(1)}, f32[6]{0:T(128)}, u32[]{:S(2)}) copy-start(f32[6]{0:T(128)} %param.22) | copy-start | bytes 76
Sparse Core Ops, SparseCore 0:
  10.9 123.7 all-gather.3

commit v5 on v4

--- a/solution.py
+++ b/solution.py
@@ -127,7 +127,8 @@
     ones_lane = lax.broadcasted_iota(jnp.int32, (TOKENS, LANES), 1) == HEAD_DIM
     v_ref[...] = jnp.where(ones_lane, 1.0, 0.0).astype(BF16)
 
-    def one_latent(l, carry):
+    def one_latent(p, m):
+        l = 2 * p + m
         ft = ft_ref[l]
         f = jnp.transpose(ft.astype(F32)).astype(BF16)
         lane = lax.broadcasted_iota(jnp.int32, (TOKENS, LANES), 1)
@@ -146,35 +147,35 @@
             scores = dot(q_ref[rows, :], kt_ref[...])
             weights = jnp.exp2(scores - jnp.max(scores, axis=1, keepdims=True)).astype(BF16)
             mixed = dot(weights, v_ref[...])
-            own_ref[l, rows, :] = (mixed / mixed[:, HEAD_DIM : HEAD_DIM + 1]).astype(BF16)
+            mixed = jnp.transpose(mixed / mixed[:, HEAD_DIM : HEAD_DIM + 1])[:HEAD_DIM]
+            for t in range(Q_ROWS // tokens):
+                own_ref[p, j * (Q_ROWS // tokens) + t, :, m * tokens : (m + 1) * tokens] = mixed[
+                    :, t * tokens : (t + 1) * tokens
+                ].astype(BF16)
             return carry
         lax.fori_loop(0, TOKENS // Q_ROWS, one_block, 0)
-        ring(me, lambda k, peer: send_out(l, k, peer).start())
-        arrived[me, l] = own_ref[l, rows_of(me), :]
+
+    def one_pair(p, carry):
+        one_latent(p, 0)
+        one_latent(p, 1)
+        ring(me, lambda k, peer: send_out(p, k, peer).start())
+        arrived[me, p] = own_ref[p, me]
         return carry
 
-    def rows_of(peer):
-        return pl.ds(pl.multiple_of(peer * tokens, tokens), tokens)
-
-    def send_out(l, k, peer):
-        return remote(
-            own_ref.at[l, rows_of(peer)], arrived.at[me, l], out_send.at[k, l], out_recv.at[me, l], {"seq": peer}
-        )
+    def send_out(p, k, peer):
+        return remote(own_ref.at[p, peer], arrived.at[me, p], out_send.at[k, p], out_recv.at[me, p], {"seq": peer})
 
     def wait_out(k, peer):
-        def one(l, carry):
+        for p in range(count // 2):
             remote(
-                own_ref.at[l, rows_of(peer)], arrived.at[peer, l], out_send.at[k, l], out_recv.at[peer, l], {"seq": peer}
+                own_ref.at[p, peer], arrived.at[peer, p], out_send.at[k, p], out_recv.at[peer, p], {"seq": peer}
             ).wait()
-            return carry
-
-        lax.fori_loop(0, count, one, 0)
-
-    lax.fori_loop(0, count, one_latent, 0)
+
+    lax.fori_loop(0, count // 2, one_pair, 0)
     ring(me, wait_out)
-    for l in range(count):
-        heads = [arrived[h, l].astype(F32)[:, :HEAD_DIM] for h in range(HEADS)]
-        out_ref[l * tokens : (l + 1) * tokens, :] = jnp.concatenate(heads, axis=1).astype(BF16)
+    for p in range(count // 2):
+        heads = jnp.concatenate([arrived[h, p].astype(F32) for h in range(HEADS)], axis=0)
+        out_ref[2 * p * tokens : 2 * (p + 1) * tokens, :] = jnp.transpose(heads).astype(BF16)
 
 
 def attend(lat, cols, patch, wq, wk, wv):
@@ -190,11 +191,11 @@
         scratch_shapes=[
             pltpu.VMEM((HEADS, count, channels, tokens), BF16),
             pltpu.VMEM((HEADS,) + cols.shape, F32),
-            pltpu.VMEM((HEADS, count, tokens, LANES), BF16),
-            pltpu.VMEM((count, TOKENS, LANES), BF16),
+            pltpu.VMEM((HEADS, count // 2, HEAD_DIM, 2 * tokens), BF16),
+            pltpu.VMEM((count // 2, HEADS, HEAD_DIM, 2 * tokens), BF16),
         ]
         + [pltpu.SemaphoreType.DMA((HEADS,))] * 4
-        + [pltpu.SemaphoreType.DMA((HEADS, count))] * 2
+        + [pltpu.SemaphoreType.DMA((HEADS, count // 2))] * 2
         + [
             pltpu.VMEM((count, BASE, TOKENS), BF16),
             pltpu.VMEM((BASE, D), F32),
@@ -214,25 +215,28 @@
 
 
 def feed_forward_kernel(
-    guidance_ref, state_ref, mods_ref, stacked_ref, out_w_ref,
-    out_ref, fc1_ref, fc2_ref, normed_ref, theirs_ref, part_ref, got_ref, total_ref, noise_ref, partner_ref,
+    guidance_ref, attended_ref, start_ref, mods_ref, stacked_ref, out_w_ref,
+    out_ref, proj_ref, fc1_ref, fc2_ref, state_ref, normed_ref, theirs_ref, part_ref, got_ref, total_ref, noise_ref, partner_ref,
     load_sem, send_sem, recv_sem,
 ):
     side = lax.axis_index("cfg")
     peer = {"cfg": 1 - side}
     count = mods_ref.shape[1]
-    tokens = state_ref.shape[0] // count
+    tokens = start_ref.shape[0] // count
     units = fc1_ref.shape[1]
     barrier = pltpu.get_barrier_semaphore()
     pl.semaphore_signal(barrier, inc=1, device_id=peer, device_id_type=MESH)
     loads = [
-        pltpu.make_async_copy(stacked_ref.at[:, n * units : (n + 1) * units, :], target, load_sem.at[n])
-        for n, target in enumerate((fc1_ref, fc2_ref))
+        pltpu.make_async_copy(stacked_ref.at[:, first : first + target.shape[1], :], target, load_sem.at[n])
+        for n, (first, target) in enumerate(((2 * units, proj_ref), (0, fc1_ref), (units, fc2_ref)))
     ]
     for load in loads:
         load.start()
+    loads[0].wait()
+    total_ref[...] = dot(attended_ref[...], proj_ref[...].reshape(D, D), NT)
     for l in range(count):
         rows = slice(l * tokens, (l + 1) * tokens)
+        state_ref[rows, :] = start_ref[rows, :] + mods_ref[2, l : l + 1, :] * total_ref[rows, :]
         normed_ref[rows, :] = (
             layer_norm(state_ref[rows, :]) * (1.0 + mods_ref[4, l : l + 1, :]) + mods_ref[3, l : l + 1, :]
         ).astype(BF16)
@@ -252,7 +256,7 @@
 
         lax.fori_loop(0, HEADS // 8, one, 0)
 
-    for load in loads:
+    for load in loads[1:]:
         load.wait()
     hand.wait()
     half_of(theirs_ref, part_ref)
@@ -278,17 +282,19 @@
     out_ref[...] = free_noise + guidance_ref[0] * (cond_noise - free_noise)
 
 
-def feed_forward(state, mods, stacked, w_out, guidance, units):
+def feed_forward(attended, state, mods, stacked, w_out, guidance, units):
     tokens = state.shape[0]
     whole = pl.BlockSpec(memory_space=pltpu.VMEM)
     return pl.pallas_call(
         feed_forward_kernel,
         out_shape=jax.ShapeDtypeStruct((8, tokens), F32),
-        in_specs=[pl.BlockSpec(memory_space=pltpu.SMEM), whole, whole, pl.BlockSpec(memory_space=pl.ANY), whole],
+        in_specs=[pl.BlockSpec(memory_space=pltpu.SMEM), whole, whole, whole, pl.BlockSpec(memory_space=pl.ANY), whole],
         out_specs=whole,
         scratch_shapes=[
+            pltpu.VMEM((HEADS, HEAD_DIM, D), BF16),
             pltpu.VMEM((HEADS, units, D), BF16),
             pltpu.VMEM((HEADS, units, D), BF16),
+            pltpu.VMEM((tokens, D), F32),
             pltpu.VMEM((tokens, D), BF16),
             pltpu.VMEM((tokens, D), BF16),
             pltpu.VMEM((tokens, D), F32),
@@ -296,13 +302,13 @@
             pltpu.VMEM((tokens, D), F32),
             pltpu.VMEM((16, tokens), F32),
             pltpu.VMEM((8, tokens), F32),
-            pltpu.SemaphoreType.DMA((2,)),
+            pltpu.SemaphoreType.DMA((3,)),
             pltpu.SemaphoreType.DMA((3,)),
             pltpu.SemaphoreType.DMA((3,)),
         ],
         compiler_params=pltpu.CompilerParams(collective_id=0, has_side_effects=True),
         cost_estimate=pl.CostEstimate(flops=8 * 10**9, bytes_accessed=12 * 10**6, transcendentals=2 * 10**6),
-    )(guidance, state, mods, stacked, w_out)
+    )(guidance, attended, state, mods, stacked, w_out)
 
 
 def shards(
@@ -316,7 +322,6 @@
     fc1_half = lax.dynamic_slice_in_dim(w_fc1.T, side * half, half, 0)
     fc2_half = lax.dynamic_slice_in_dim(w_fc2, side * half, half, 0)
     stacked = lax.all_gather(jnp.concatenate([fc1_half, fc2_half, w_proj.T], axis=0), "seq", axis=0)
-    proj_full = stacked[:, 2 * half :].reshape(D, D)
 
     classes = jnp.where(side == 0, labels, CLASSES)
     steps_all = lax.all_gather(timesteps, "lat", axis=0, tiled=True)
@@ -344,9 +349,7 @@
     lines = lax.dynamic_slice_in_dim(pos, GRID + place * (tok_count // GRID), tok_count // GRID, 0)
     own_pos = (columns[None] + lines[:, None]).reshape(tok_count, D)
     state = dot(latents.reshape(-1, channels).astype(BF16), w_patch).reshape(count, tok_count, D) + own_pos[None]
-    projected = dot(attended, proj_full, NT).reshape(count, tok_count, D)
-    state = state + mods[2][:, None, :] * projected
-    guided = feed_forward(state.reshape(-1, D), mods, stacked, w_out, guidance, half)
+    guided = feed_forward(attended, state.reshape(-1, D), mods, stacked, w_out, guidance, half)
     half_width = channels // 2
     own_latent = lax.dynamic_slice_in_dim(latents, side * half_width, half_width, 2)
     guided = guided.T.reshape(count, tok_count, half_width)

time: 169 us -> 159 us (0.941)
  Pallas kernels: 85.9 us -> 83 us
  local copies, waits for them, and re-layouts: 11.5 us -> 8.64 us
  waiting for transfers between devices: 11.7 us -> 9.84 us
    pallas_call x1, Pallas kernels: 65.9 us -> 60.9 us  [attend(): pl.pallas_call(attend_kernel, out_shape=(jax.ShapeDtypeStruct((count * to...]
    pallas_call x1, Pallas kernels: 20 us -> 22.1 us  [feed_forward(): pl.pallas_call(feed_forward_kernel, out_shape=jax.ShapeDtypeStruct((8, to...]
    slice x1 -> x0, local copies, waits for them, and re-layouts: 2.03 us -> none  [shards(): proj_full = stacked[:, 2 * half:].reshape(D, D)]
    dot_general x5 -> x4, matrix products: 7.22 us -> 5.83 us  [dot(): lax.dot_general(a, b, dims, precision=precision, preferred_element_type=F32)]
  transfers between devices with their start and end apart: 5 -> 5, of which waited for: 2 -> 1; matrix products, arithmetic and copies ran while one was open for 7% -> 8% of each run, Pallas kernels for 39% -> 38%
where the time goes in v5:
time: 159 us
  Pallas kernels  83 us (52%)
  blocking collectives  17.5 us (11%)
  between operations  14.9 us (9%)
  starting transfers between devices  14.3 us (9%)
  waiting for transfers between devices  9.84 us (6%)
  local copies, waits for them, and re-layouts  8.64 us (5%)
  matrix products  5.83 us (4%)
  other arithmetic  4.72 us (3%)
    pallas_call x1, Pallas kernels, attend(): pl.pallas_call(attend_kernel, out_shape=(jax.ShapeDtypeStruct((count * to...  60.9 us
    pallas_call x1, Pallas kernels, feed_forward(): pl.pallas_call(feed_forward_kernel, out_shape=jax.ShapeDtypeStruct((8, to...  22.1 us
    ppermute x3, starting transfers between devices, shards(): lax.ppermute(blocks[j], 'seq', [(s, (3 * s + j) % HEADS) for s in range(H...  11.1 us
    all_gather x1, blocking collectives, shards(): hidden_time = lax.all_gather(hidden_own, 'lat', axis=1, tiled=True)  10.2 us
    all_gather x1, waiting for transfers between devices, shards(): lax.all_gather(jnp.concatenate([fc1_half, fc2_half, w_proj.T], axis=0), '...  9.81 us
    unnamed x1, blocking collectives  7.25 us
    dot_general x4, matrix products, dot(): lax.dot_general(a, b, dims, precision=precision, preferred_element_type=F32)  5.83 us
    all_to_all x1, starting transfers between devices, shards(): lax.all_to_all(vector_own, 'lat', split_axis=0, concat_axis=1, tiled=True)  3.27 us
  transfers between devices with their start and end apart: 5, of which 1 were waited for; matrix products, arithmetic and copies ran while one was open for 8% of the time, Pallas kernels for 38%

profile of v5, /device:TPU:1, one launch (start us, length us, event | category | flops | bytes accessed | tf_op | source)
XLA Modules:
  0.0 158.8 jit_solution(10588431883478796116)
XLA Ops:
  6.5 1.2 constant_dynamic-slice_fusion
  7.7 1.0 dynamic-slice_bitcast_fusion
  8.7 2.0 %pad_maximum_fusion = bf16[360,1152]{1,0:T(8,128)(2,1)} fusion(bf16[72,1152]{1,0:T(8,128)(2,1)} %bitcast.41, bf16[144,1152]{1,0:T(8,128)(2,1)S(1)} %constant_dynamic-slice_fusion, bf16[144,1152]{1,0:T(8,128)(2,1)S(1)} %dynamic-slice_bitcast_fusion), kind=kLoop, calls=%fused_computation.2 | loop fusion | flops 2488320 | bytes 1658880 | tf_op jit(solution)/shard_map/concatenate | solution.py:324
  10.7 0.8 fusion.18
  11.6 1.7 %collective-permute-start = (bf16[72,1152]{1,0:T(8,128)(2,1)}, bf16[72,1152]{1,0:T(8,128)(2,1)S(1)}, u32[]{:S(2)}, u32[]{:S(2)}) collective-permute-start(bf16[72,1152]{1,0:T(8,128)(2,1)} %get-tuple-element.12), channel_id=1, source_target_pairs={{0,0},{1,3},{2,6},{3,9},{4,12},{5,15},{6,2},{7,5},{8,8},{9,11},{10... | collective-permute-start | bytes 497672 | tf_op jit(solution)/shard_map/ppermute | solution.py:340
  13.3 4.6 %collective-permute-start.1 = (bf16[72,1152]{1,0:T(8,128)(2,1)}, bf16[72,1152]{1,0:T(8,128)(2,1)S(1)}, u32[]{:S(2)}, u32[]{:S(2)}) collective-permute-start(bf16[72,1152]{1,0:T(8,128)(2,1)} %get-tuple-element.14), channel_id=1, source_target_pairs={{0,1},{1,4},{2,7},{3,10},{4,13},{5,0},{6,3},{7,6},{8,9},{9,12},{10... | collective-permute-start | bytes 497672 | tf_op jit(solution)/shard_map/ppermute | solution.py:340
  17.8 4.8 %collective-permute-start.2 = (bf16[72,1152]{1,0:T(8,128)(2,1)}, bf16[72,1152]{1,0:T(8,128)(2,1)}, u32[]{:S(2)}, u32[]{:S(2)}) collective-permute-start(bf16[72,1152]{1,0:T(8,128)(2,1)} %get-tuple-element.13), channel_id=1, source_target_pairs={{0,2},{1,5},{2,8},{3,11},{4,14},{5,1},{6,4},{7,7},{8,10},{9,13},{1... | collective-permute-start | bytes 497672 | tf_op jit(solution)/shard_map/ppermute | solution.py:340
  22.7 0.6 dynamic-slice.4
  23.9 0.2 dynamic-update-slice
  24.2 7.3 %all-reduce = s32[24]{0:T(128)S(1)} all-reduce(s32[24]{0:T(128)S(1)} %dynamic-update-slice), channel_id=1, replica_groups=mesh['cfg'=2,'lat'=4,'seq'=16] {'lat'}, use_global_device_ids=true, to_apply=%add | all-reduce | flops 24 | bytes 192
  31.4 0.1 fusion.7
  31.6 1.1 fusion.4
  32.7 10.2 %all-gather.1 = bf16[4,288,24]{1,2,0:T(8,128)(2,1)S(1)} all-gather(bf16[1,288,24]{1,2,0:T(8,128)(2,1)S(1)} %fusion.4), channel_id=1, replica_groups=mesh['cfg'=2,'lat'=4,'seq'=16] {'lat'}, dimensions={0}, use_global_device_ids=true | all-gather | bytes 69120 | tf_op jit(solution)/shard_map/all_gather | solution.py:330
  42.9 0.1 reshape.51
  43.1 0.3 fusion.19
  43.4 0.6 all_to_all.14
  44.0 3.3 %all-to-all-start = ((f32[4,6,288]{2,1,0:T(8,128)}), f32[4,6,288]{2,1,0:T(8,128)S(1)}, u32[]{:S(2)}, u32[]{:S(2)}) async-start(f32[4,6,288]{2,1,0:T(8,128)} %all_to_all.14), calls=%async_computation | async-start | bytes 98304 | tf_op jit(solution)/shard_map/all_to_all | solution.py:332
  47.3 0.8 constant_dynamic-slice_fusion.1
  48.1 0.6 convert_bitcast_fusion.lat_ref
  48.7 0.9 broadcast_add_fusion
  49.7 1.6 %convolution_add_fusion = f32[6,64,1152]{2,1,0:T(8,128)} fusion(f32[64,1152]{1,0:T(8,128)S(1)} %bitcast.38, bf16[16,1152]{1,0:T(8,128)(2,1)S(1)} %copy-done.5, f32[6,64,16]{1,2,0:T(8,128)S(1)} %copy-done.3), kind=kOutput, calls=%fused_computation | convolution fusion | flops 14604288 | bytes 2125824 | tf_op jit(solution)/shard_map/dot_general | solution.py:42
  51.3 0.9 copy.30.out_w_ref
  52.9 0.1 all_to_all.17
  53.0 2.7 %fusion.1.cols_ref = f32[6,576]{1,0:T(8,128)} fusion(bf16[1152,576]{0,1:T(8,128)(2,1)} %param.28, f32[6,1152]{1,0:T(8,128)S(1)} %all_to_all.17, bf16[1001,1152]{1,0:T(8,128)(2,1)S(1)} %copy-done, s32[6]{0:T(128)S(1)} %broadcast_select_fusion), kind=kOutput, calls=%fused_computation.11 | convolution fusion | flops 21847926 | bytes 3674904 | tf_op jit(solution)/shard_map/dot_general | solution.py:42
  55.8 1.0 pad_maximum_fusion.1
  56.8 0.8 dynamic-slice_bitcast_fusion.1
  57.6 60.9 %shard_map.172 = (bf16[384,1152]{1,0:T(8,128)(2,1)}, f32[8,6,1152]{2,1,0:T(8,128)}) custom-call(bf16[6,16,64]{2,1,0:T(8,128)(2,1)} %convert_bitcast_fusion.lat_ref, f32[6,576]{1,0:T(8,128)} %fusion.1.cols_ref, bf16[16,1152]{1,0:T(8,128)(2,1)} %patch_ref.1, f32[64,1152]{1,0:T(8,128)} %constant.64.clone.pos_ref, bf16[72,1152]{1,0:T(8,128)(2,1)} %get-tuple-element.11.wq_ref, ...), custom_call_target="tpu_custom_call" | custom-call | flops 8000000000 | bytes 4000000 | tf_op jit(solution)/shard_map/pallas_call | solution.py:186
  118.5 9.8 %all-gather.4.cloned.1.call-done = bf16[5760,1152]{1,0:T(8,128)(2,1)} async-done(((bf16[360,1152]{1,0:T(8,128)(2,1)}), bf16[5760,1152]{1,0:T(8,128)(2,1)}) %all-gather.4.cloned.1.call-update) | async-done | bytes 13271056 | tf_op jit(solution)/shard_map/all_gather | solution.py:324
  128.4 22.1 %shard_map.173 = f32[8,384]{1,0:T(8,128)} custom-call(f32[1]{0:T(128)S(6)} %copy.37.guidance_ref, bf16[384,1152]{1,0:T(8,128)(2,1)} %get-tuple-element.7.attended_ref, f32[384,1152]{1,0:T(8,128)} %bitcast.37, f32[8,6,1152]{2,1,0:T(8,128)} %get-tuple-element.8.mods_ref, bf16[16,360,1152]{2,1,0:T(8,128)(2,1)} %bitcast.45, bf16[1152,16]{1,0:T(8,128)(2,1)} %copy.30.out_w_ref), custom_call_target="tpu_custom_call" | custom-call | flops 8000000000 | bytes 12000000 | tf_op jit(solution)/shard_map/pallas_call | solution.py:288
  150.5 0.8 reshape.45
  151.2 0.1 fusion.2
  151.3 0.6 copy.31
  (35 shorter events, 0.1 us)
Async XLA Ops:
  6.5 46.5 %copy-start = (bf16[1001,1152]{1,0:T(8,128)(2,1)S(1)}, bf16[1001,1152]{1,0:T(8,128)(2,1)}, u32[]{:S(2)}) copy-start(bf16[1001,1152]{1,0:T(8,128)(2,1)} %param.25) | copy-start | bytes 6918916
  6.5 121.8 %all-gather.4.cloned.1.call-start = ((), (), s32[]{:S(2)}) async-start(), calls=%async_computation.1 | async-start | bytes 14100480 | tf_op jit(solution)/shard_map/all_gather | solution.py:324
  6.5 4.2 %copy-start.2 = (bf16[1152,216]{0,1:T(8,128)(2,1)S(1)}, bf16[1152,216]{0,1:T(8,128)(2,1)}, u32[]{:S(2)}) copy-start(bf16[1152,216]{0,1:T(8,128)(2,1)} %param.29) | copy-start | bytes 1492996
  8.7 13.9 %copy-start.10 = (u32[128]{0:T(128)S(1)}, u32[128]{0:T(128)}, u32[]{:S(2)}) copy-start(u32[128]{0:T(128)} %constant.76) | copy-start | bytes 1540
  8.7 15.2 %copy-start.8 = (s32[6]{0:T(128)S(1)}, s32[6]{0:T(128)}, u32[]{:S(2)}) copy-start(s32[6]{0:T(128)} %param.19) | copy-start | bytes 76
  8.7 34.3 %copy-start.1 = (bf16[1152,288]{0,1:T(8,128)(2,1)S(1)}, bf16[1152,288]{0,1:T(8,128)(2,1)}, u32[]{:S(2)}) copy-start(bf16[1152,288]{0,1:T(8,128)(2,1)} %param.27) | copy-start | bytes 1990660
  10.7 36.6 %copy-start.9 = (s32[6]{0:T(128)S(1)}, s32[6]{0:T(128)}, u32[]{:S(2)}) copy-start(s32[6]{0:T(128)} %param.20) | copy-start | bytes 76
  10.7 37.4 %copy-start.3 = (f32[6,64,16]{1,2,0:T(8,128)S(1)}, f32[6,64,16]{1,2,0:T(8,128)}, u32[]{:S(2)}) copy-start(f32[6,64,16]{1,2,0:T(8,128)} %param.18) | copy-start | bytes 73732
  11.6 38.1 %copy-start.5 = (bf16[16,1152]{1,0:T(8,128)(2,1)S(1)}, bf16[16,1152]{1,0:T(8,128)(2,1)}, u32[]{:S(2)}) copy-start(bf16[16,1152]{1,0:T(8,128)(2,1)} %patch_ref.1) | copy-start | bytes 110596
  11.6 44.2 %collective-permute-start = (bf16[72,1152]{1,0:T(8,128)(2,1)}, bf16[72,1152]{1,0:T(8,128)(2,1)S(1)}, u32[]{:S(2)}, u32[]{:S(2)}) collective-permute-start(bf16[72,1152]{1,0:T(8,128)(2,1)} %get-tuple-element.12), channel_id=1, source_target_pairs={{0,0},{1,3},{2,6},{3,9},{4,12},{5,15},{6,2},{7,5},{8,8},{9,11},{10... | collective-permute-start | bytes 497672 | tf_op jit(solution)/shard_map/ppermute | solution.py:340
  13.3 42.5 %collective-permute-start.1 = (bf16[72,1152]{1,0:T(8,128)(2,1)}, bf16[72,1152]{1,0:T(8,128)(2,1)S(1)}, u32[]{:S(2)}, u32[]{:S(2)}) collective-permute-start(bf16[72,1152]{1,0:T(8,128)(2,1)} %get-tuple-element.14), channel_id=1, source_target_pairs={{0,1},{1,4},{2,7},{3,10},{4,13},{5,0},{6,3},{7,6},{8,9},{9,12},{10... | collective-permute-start | bytes 497672 | tf_op jit(solution)/shard_map/ppermute | solution.py:340
  17.8 38.0 %collective-permute-start.2 = (bf16[72,1152]{1,0:T(8,128)(2,1)}, bf16[72,1152]{1,0:T(8,128)(2,1)}, u32[]{:S(2)}, u32[]{:S(2)}) collective-permute-start(bf16[72,1152]{1,0:T(8,128)(2,1)} %get-tuple-element.13), channel_id=1, source_target_pairs={{0,2},{1,5},{2,8},{3,11},{4,14},{5,1},{6,4},{7,7},{8,10},{9,13},{1... | collective-permute-start | bytes 497672 | tf_op jit(solution)/shard_map/ppermute | solution.py:340
  43.1 8.3 %copy-start.4 = (bf16[1152,16]{0,1:T(8,128)(2,1)S(1)}, bf16[1152,16]{0,1:T(8,128)(2,1)}, u32[]{:S(2)}) copy-start(bf16[1152,16]{0,1:T(8,128)(2,1)} %param.33) | copy-start | bytes 110596
  44.0 8.9 %all-to-all-start = ((f32[4,6,288]{2,1,0:T(8,128)}), f32[4,6,288]{2,1,0:T(8,128)S(1)}, u32[]{:S(2)}, u32[]{:S(2)}) async-start(f32[4,6,288]{2,1,0:T(8,128)} %all_to_all.14), calls=%async_computation | async-start | bytes 98304 | tf_op jit(solution)/shard_map/all_to_all | solution.py:332
  128.4 22.9 %copy-start.6 = (f32[6]{0:T(128)S(1)}, f32[6]{0:T(128)}, u32[]{:S(2)}) copy-start(f32[6]{0:T(128)} %param.23) | copy-start | bytes 76
  128.4 22.9 %copy-start.7 = (f32[6]{0:T(128)S(1)}, f32[6]{0:T(128)}, u32[]{:S(2)}) copy-start(f32[6]{0:T(128)} %param.22) | copy-start | bytes 76
Sparse Core Ops, SparseCore 0:
  10.9 117.4 all-gather.3

commit v6 on v5

--- a/solution.py
+++ b/solution.py
@@ -76,8 +76,8 @@
     lat_all, cols_all, arrived, own_ref, lat_send, lat_recv, cols_send, cols_recv, out_send, out_recv,
     ft_ref, base_ref, xs_ref, tq_ref, tv_ref, tk_ref, rstd_ref, rcol_ref, q_ref, v_ref, kt_ref,
 ):
-    count = lat_ref.shape[0]
-    tokens = lat_ref.shape[2]
+    count = cols_ref.shape[0]
+    tokens = lat_ref.shape[2] // 2
     me = lax.axis_index("seq")
     barrier = pltpu.get_barrier_semaphore()
     ring(me, lambda k, peer: pl.semaphore_signal(barrier, inc=1, device_id={"seq": peer}, device_id_type=MESH))
@@ -108,7 +108,8 @@
         mods_ref[n] = jnp.concatenate([cols_all[2 * n], cols_all[2 * n + 1]], axis=1)
     for l in range(count):
         for n in range(HEADS // 2):
-            pair = [lat_all[2 * n + m, l].astype(F32) for m in range(2)]
+            side = slice(l % 2 * tokens, (l % 2 + 1) * tokens)
+            pair = [lat_all[2 * n + m, l // 2].astype(F32)[:, side] for m in range(2)]
             ft_ref[l, :16, n * LANES : (n + 1) * LANES] = jnp.concatenate(pair, axis=1).astype(BF16)
         ft_ref[l, 16:, :] = hot
         ft = ft_ref[l].astype(F32)
@@ -179,7 +180,8 @@
 
 
 def attend(lat, cols, patch, wq, wk, wv):
-    count, channels, tokens = lat.shape
+    count = cols.shape[0]
+    tokens = lat.shape[2] // 2
     pos = position_rows()
     centred = jnp.asarray((pos - pos.mean(axis=1, keepdims=True)).astype(np.float32))
     vmem = pl.BlockSpec(memory_space=pltpu.VMEM)
@@ -189,7 +191,7 @@
         in_specs=[vmem] * 7,
         out_specs=(vmem, vmem),
         scratch_shapes=[
-            pltpu.VMEM((HEADS, count, channels, tokens), BF16),
+            pltpu.VMEM((HEADS,) + lat.shape, BF16),
             pltpu.VMEM((HEADS,) + cols.shape, F32),
             pltpu.VMEM((HEADS, count // 2, HEAD_DIM, 2 * tokens), BF16),
             pltpu.VMEM((count // 2, HEADS, HEAD_DIM, 2 * tokens), BF16),
@@ -319,9 +321,8 @@
     side = lax.axis_index("cfg")
     place = lax.axis_index("seq")
     half = w_fc2.shape[0] // 2
-    fc1_half = lax.dynamic_slice_in_dim(w_fc1.T, side * half, half, 0)
-    fc2_half = lax.dynamic_slice_in_dim(w_fc2, side * half, half, 0)
-    stacked = lax.all_gather(jnp.concatenate([fc1_half, fc2_half, w_proj.T], axis=0), "seq", axis=0)
+    parts = [jnp.concatenate([w_fc1.T[n : n + half], w_fc2[n : n + half], w_proj.T], axis=0) for n in (0, half)]
+    stacked = lax.all_gather(jnp.where(side == 0, parts[0], parts[1]), "seq", axis=0)
 
     classes = jnp.where(side == 0, labels, CLASSES)
     steps_all = lax.all_gather(timesteps, "lat", axis=0, tiled=True)
@@ -342,7 +343,7 @@
         ]
     )
     head_w = [lax.dynamic_index_in_dim(got, (HEADS * kind + place) % 3, 0, False) for kind in range(3)]
-    attended, mods = attend(lat_t, own_columns, w_patch, *head_w)
+    attended, mods = attend(jnp.concatenate([lat_t[0::2], lat_t[1::2]], axis=2), own_columns, w_patch, *head_w)
 
     pos = jnp.asarray(position_rows().astype(np.float32))
     columns = pos[:GRID]

time: 159 us -> 156 us (0.981)
  Pallas kernels: 83 us -> 73.8 us
  waiting for transfers between devices: 9.84 us -> 12.7 us
    pallas_call x1, Pallas kernels: 60.9 us -> 52.1 us  [attend(): pl.pallas_call(attend_kernel, out_shape=(jax.ShapeDtypeStruct((count * to...]
    all_gather x1, waiting for transfers between devices: 9.81 us -> 12.6 us  [shards(): lax.all_gather(jnp.where(side == 0, parts[0], parts[1]), 'seq', axis=0)]
    dynamic_slice x2 -> x0, local copies, waits for them, and re-layouts: 2.16 us -> none  [the longest x1 1.15 us: shards(): fc2_half = lax.dynamic_slice_in_dim(w_fc2, side * half, half, 0)]
    unnamed x27 -> x29, local copies, waits for them, and re-layouts: 1.89 us -> 3.41 us
  transfers between devices with their start and end apart: 5 -> 5, of which waited for: 1 -> 1; matrix products, arithmetic and copies ran while one was open for 8% -> 10% of each run, Pallas kernels for 38% -> 34%
where the time goes in v6:
time: 156 us; the launch traced here: 155 us
  Pallas kernels  73.8 us (47%)
  blocking collectives  17.1 us (11%)
  starting transfers between devices  15.3 us (10%)
  between operations  14.9 us (10%)
  waiting for transfers between devices  12.7 us (8%)
  local copies, waits for them, and re-layouts  10.2 us (7%)
  matrix products  7.27 us (5%)
  other arithmetic  3.98 us (3%)
    pallas_call x1, Pallas kernels, attend(): pl.pallas_call(attend_kernel, out_shape=(jax.ShapeDtypeStruct((count * to...  52.1 us
    pallas_call x1, Pallas kernels, feed_forward(): pl.pallas_call(feed_forward_kernel, out_shape=jax.ShapeDtypeStruct((8, to...  21.7 us
    all_gather x1, waiting for transfers between devices, shards(): lax.all_gather(jnp.where(side == 0, parts[0], parts[1]), 'seq', axis=0)  12.6 us
    ppermute x3, starting transfers between devices, shards(): lax.ppermute(blocks[j], 'seq', [(s, (3 * s + j) % HEADS) for s in range(H...  12.1 us
    all_gather x1, blocking collectives, shards(): hidden_time = lax.all_gather(hidden_own, 'lat', axis=1, tiled=True)  9.4 us
    unnamed x1, blocking collectives  7.69 us
    dot_general x4, matrix products, dot(): lax.dot_general(a, b, dims, precision=precision, preferred_element_type=F32)  7.27 us
    unnamed x29, local copies, waits for them, and re-layouts  3.41 us
  transfers between devices with their start and end apart: 5, of which 1 were waited for; matrix products, arithmetic and copies ran while one was open for 10% of the time, Pallas kernels for 34%

profile of v6, /device:TPU:1, one launch (start us, length us, event | category | flops | bytes accessed | tf_op | source)
XLA Modules:
  0.0 155.2 jit_solution(311993567175279223)
XLA Ops:
  6.5 1.5 slice_bitcast_fusion
  8.1 1.1 fusion
  9.2 0.0 all-gather.3.cloned.1.call-update
  9.3 0.6 dynamic-slice
  10.5 0.2 dynamic-update-slice
  10.8 7.7 %all-reduce = s32[24]{0:T(128)S(1)} all-reduce(s32[24]{0:T(128)S(1)} %dynamic-update-slice), channel_id=1, replica_groups=mesh['cfg'=2,'lat'=4,'seq'=16] {'lat'}, use_global_device_ids=true, to_apply=%add | all-reduce | flops 24 | bytes 192
  18.5 0.1 fusion.8
  18.6 1.1 fusion.5
  19.7 9.4 %all-gather = bf16[4,288,24]{1,2,0:T(8,128)(2,1)S(1)} all-gather(bf16[1,288,24]{1,2,0:T(8,128)(2,1)S(1)} %fusion.5), channel_id=1, replica_groups=mesh['cfg'=2,'lat'=4,'seq'=16] {'lat'}, dimensions={0}, use_global_device_ids=true | all-gather | bytes 69120 | tf_op jit(solution)/shard_map/all_gather | solution.py:331
  29.1 0.7 copy.28
  29.8 1.6 %reshape.131 = bf16[1152,24]{0,1:T(8,128)(2,1)} reshape(bf16[4,288,24]{1,0,2:T(4,128)(2,1)} %copy.28) | data formatting | bytes 110592
  31.4 1.8 %fusion.21 = f32[24,288]{1,0:T(8,128)} fusion(bf16[1152,24]{0,1:T(8,128)(2,1)} %reshape.131, bf16[1152,288]{0,1:T(8,128)(2,1)S(1)} %copy-done.1), kind=kOutput, calls=%fused_computation.43 | convolution fusion | flops 15925248 | bytes 746496 | tf_op jit(solution)/shard_map/dot_general | solution.py:42
  33.2 1.4 all_to_all.14
  34.6 3.3 %all-to-all-start = ((f32[4,6,288]{2,1,0:T(8,128)}), f32[4,6,288]{2,1,0:T(8,128)S(1)}, u32[]{:S(2)}, u32[]{:S(2)}) async-start(f32[4,6,288]{2,1,0:T(8,128)} %all_to_all.14), calls=%async_computation | async-start | bytes 98304 | tf_op jit(solution)/shard_map/all_to_all | solution.py:333
  37.9 0.7 collective-permute-start
  38.6 7.3 %collective-permute-start.2 = (bf16[72,1152]{1,0:T(8,128)(2,1)S(1)}, bf16[72,1152]{1,0:T(8,128)(2,1)S(1)}, u32[]{:S(2)}, u32[]{:S(2)}) collective-permute-start(bf16[72,1152]{1,0:T(8,128)(2,1)S(1)} %get-tuple-element.17), channel_id=1, source_target_pairs={{0,2},{1,5},{2,8},{3,11},{4,14},{5,1},{6,4},{7,7},{8,10},{9,13},{1... | collective-permute-start | bytes 497672 | tf_op jit(solution)/shard_map/ppermute | solution.py:341
  45.9 4.1 %collective-permute-start.1 = (bf16[72,1152]{1,0:T(8,128)(2,1)S(1)}, bf16[72,1152]{1,0:T(8,128)(2,1)}, u32[]{:S(2)}, u32[]{:S(2)}) collective-permute-start(bf16[72,1152]{1,0:T(8,128)(2,1)S(1)} %get-tuple-element.18), channel_id=1, source_target_pairs={{0,1},{1,4},{2,7},{3,10},{4,13},{5,0},{6,3},{7,6},{8,9},{9,12},{10... | collective-permute-start | bytes 497672 | tf_op jit(solution)/shard_map/ppermute | solution.py:341
  50.0 0.8 constant_dynamic-slice_fusion
  50.8 1.0 broadcast_add_fusion
  51.8 1.7 %convolution_add_fusion = f32[6,64,1152]{2,1,0:T(8,128)} fusion(f32[64,1152]{1,0:T(8,128)S(1)} %bitcast.46, bf16[16,1152]{1,0:T(8,128)(2,1)S(1)} %copy-done.6, f32[6,64,16]{1,2,0:T(8,128)S(1)} %copy-done.3), kind=kOutput, calls=%fused_computation | convolution fusion | flops 14604288 | bytes 2125824 | tf_op jit(solution)/shard_map/dot_general | solution.py:42
  53.5 0.7 pad_maximum_fusion.3.lat_ref
  54.8 0.9 copy.30.out_w_ref
  55.8 0.1 all_to_all.17
  55.9 2.7 %fusion.2.cols_ref = f32[6,576]{1,0:T(8,128)} fusion(bf16[1152,576]{0,1:T(8,128)(2,1)} %param.28, f32[6,1152]{1,0:T(8,128)S(1)} %all_to_all.17, bf16[1001,1152]{1,0:T(8,128)(2,1)S(1)} %copy-done, s32[6]{0:T(128)S(1)} %broadcast_select_fusion), kind=kOutput, calls=%fused_computation.16 | convolution fusion | flops 21847926 | bytes 3674904 | tf_op jit(solution)/shard_map/dot_general | solution.py:42
  58.6 1.0 pad_maximum_fusion.2
  59.6 0.8 dynamic-slice_bitcast_fusion
  60.4 52.1 %shard_map.172 = (bf16[384,1152]{1,0:T(8,128)(2,1)}, f32[8,6,1152]{2,1,0:T(8,128)}) custom-call(bf16[3,16,128]{2,1,0:T(8,128)(2,1)} %pad_maximum_fusion.3.lat_ref, f32[6,576]{1,0:T(8,128)} %fusion.2.cols_ref, bf16[16,1152]{1,0:T(8,128)(2,1)} %patch_ref.1, f32[64,1152]{1,0:T(8,128)} %constant.60.clone.pos_ref, bf16[72,1152]{1,0:T(8,128)(2,1)} %get-tuple-element.15.wq_ref, ...), custom_call_target="tpu_custom_call" | custom-call | flops 8000000000 | bytes 4000000 | tf_op jit(solution)/shard_map/pallas_call | solution.py:188
  112.6 12.6 %all-gather.3.cloned.1.call-done.stacked_ref = bf16[16,360,1152]{2,1,0:T(8,128)(2,1)} async-done(((bf16[1,360,1152]{2,1,0:T(8,128)(2,1)}), bf16[16,360,1152]{2,1,0:T(8,128)(2,1)}) %all-gather.3.cloned.1.call-update) | async-done | bytes 13271056 | tf_op jit(solution)/shard_map/all_gather | solution.py:325
  125.2 21.7 %shard_map.173 = f32[8,384]{1,0:T(8,128)} custom-call(f32[1]{0:T(128)S(6)} %copy.37.guidance_ref, bf16[384,1152]{1,0:T(8,128)(2,1)} %get-tuple-element.7.attended_ref, f32[384,1152]{1,0:T(8,128)} %bitcast.45, f32[8,6,1152]{2,1,0:T(8,128)} %get-tuple-element.8.mods_ref, bf16[16,360,1152]{2,1,0:T(8,128)(2,1)} %all-gather.3.cloned.1.call-done.stacked_ref, ...), custom_call_target="tpu_custom_call" | custom-call | flops 8000000000 | bytes 12000000 | tf_op jit(solution)/shard_map/pallas_call | solution.py:290
  146.9 0.8 reshape.126
  147.7 0.1 fusion.3
  147.7 0.6 copy.31
  (38 shorter events, 0.2 us)
Async XLA Ops:
  6.5 49.3 %copy-start = (bf16[1001,1152]{1,0:T(8,128)(2,1)S(1)}, bf16[1001,1152]{1,0:T(8,128)(2,1)}, u32[]{:S(2)}) copy-start(bf16[1001,1152]{1,0:T(8,128)(2,1)} %param.25) | copy-start | bytes 6918916
  6.5 1.6 %copy-start.4 = (bf16[1152,72]{0,1:T(8,128)(2,1)S(1)}, bf16[1152,72]{0,1:T(8,128)(2,1)}, u32[]{:S(2)}) copy-start(bf16[1152,72]{0,1:T(8,128)(2,1)} %param.30) | copy-start | bytes 497668
  6.5 118.6 %all-gather.3.cloned.1.call-start = ((), (), s32[]{:S(2)}) async-start(), calls=%async_computation.1 | async-start | bytes 14100480 | tf_op jit(solution)/shard_map/all_gather | solution.py:325
  8.1 1.2 copy-start.11
  8.1 2.4 %copy-start.9 = (s32[6]{0:T(128)S(1)}, s32[6]{0:T(128)}, u32[]{:S(2)}) copy-start(s32[6]{0:T(128)} %param.19) | copy-start | bytes 76
  8.1 23.3 %copy-start.1 = (bf16[1152,288]{0,1:T(8,128)(2,1)S(1)}, bf16[1152,288]{0,1:T(8,128)(2,1)}, u32[]{:S(2)}) copy-start(bf16[1152,288]{0,1:T(8,128)(2,1)} %param.27) | copy-start | bytes 1990660
  9.2 28.6 %copy-start.2 = (bf16[1152,216]{0,1:T(8,128)(2,1)S(1)}, bf16[1152,216]{0,1:T(8,128)(2,1)}, u32[]{:S(2)}) copy-start(bf16[1152,216]{0,1:T(8,128)(2,1)} %param.29) | copy-start | bytes 1492996
  9.2 40.8 %copy-start.3 = (f32[6,64,16]{1,2,0:T(8,128)S(1)}, f32[6,64,16]{1,2,0:T(8,128)}, u32[]{:S(2)}) copy-start(f32[6,64,16]{1,2,0:T(8,128)} %param.18) | copy-start | bytes 73732
  9.2 40.8 %copy-start.10 = (s32[6]{0:T(128)S(1)}, s32[6]{0:T(128)}, u32[]{:S(2)}) copy-start(s32[6]{0:T(128)} %param.20) | copy-start | bytes 76
  33.2 18.7 %copy-start.6 = (bf16[16,1152]{1,0:T(8,128)(2,1)S(1)}, bf16[16,1152]{1,0:T(8,128)(2,1)}, u32[]{:S(2)}) copy-start(bf16[16,1152]{1,0:T(8,128)(2,1)} %patch_ref.1) | copy-start | bytes 110596
  34.6 21.2 %all-to-all-start = ((f32[4,6,288]{2,1,0:T(8,128)}), f32[4,6,288]{2,1,0:T(8,128)S(1)}, u32[]{:S(2)}, u32[]{:S(2)}) async-start(f32[4,6,288]{2,1,0:T(8,128)} %all_to_all.14), calls=%async_computation | async-start | bytes 98304 | tf_op jit(solution)/shard_map/all_to_all | solution.py:333
  37.9 16.9 %copy-start.5 = (bf16[1152,16]{0,1:T(8,128)(2,1)S(1)}, bf16[1152,16]{0,1:T(8,128)(2,1)}, u32[]{:S(2)}) copy-start(bf16[1152,16]{0,1:T(8,128)(2,1)} %param.33) | copy-start | bytes 110596
  37.9 20.7 %collective-permute-start = (bf16[72,1152]{1,0:T(8,128)(2,1)S(1)}, bf16[72,1152]{1,0:T(8,128)(2,1)S(1)}, u32[]{:S(2)}, u32[]{:S(2)}) collective-permute-start(bf16[72,1152]{1,0:T(8,128)(2,1)S(1)} %get-tuple-element.16), channel_id=1, source_target_pairs={{0,0},{1,3},{2,6},{3,9},{4,12},{5,15},{6,2},{7,5},{8,8},{9,11},{10... | collective-permute-start | bytes 497672 | tf_op jit(solution)/shard_map/ppermute | solution.py:341
  38.6 20.0 %collective-permute-start.2 = (bf16[72,1152]{1,0:T(8,128)(2,1)S(1)}, bf16[72,1152]{1,0:T(8,128)(2,1)S(1)}, u32[]{:S(2)}, u32[]{:S(2)}) collective-permute-start(bf16[72,1152]{1,0:T(8,128)(2,1)S(1)} %get-tuple-element.17), channel_id=1, source_target_pairs={{0,2},{1,5},{2,8},{3,11},{4,14},{5,1},{6,4},{7,7},{8,10},{9,13},{1... | collective-permute-start | bytes 497672 | tf_op jit(solution)/shard_map/ppermute | solution.py:341
  45.9 12.7 %collective-permute-start.1 = (bf16[72,1152]{1,0:T(8,128)(2,1)S(1)}, bf16[72,1152]{1,0:T(8,128)(2,1)}, u32[]{:S(2)}, u32[]{:S(2)}) collective-permute-start(bf16[72,1152]{1,0:T(8,128)(2,1)S(1)} %get-tuple-element.18), channel_id=1, source_target_pairs={{0,1},{1,4},{2,7},{3,10},{4,13},{5,0},{6,3},{7,6},{8,9},{9,12},{10... | collective-permute-start | bytes 497672 | tf_op jit(solution)/shard_map/ppermute | solution.py:341
  125.2 22.5 %copy-start.7 = (f32[6]{0:T(128)S(1)}, f32[6]{0:T(128)}, u32[]{:S(2)}) copy-start(f32[6]{0:T(128)} %param.23) | copy-start | bytes 76
  125.2 22.5 %copy-start.8 = (f32[6]{0:T(128)S(1)}, f32[6]{0:T(128)}, u32[]{:S(2)}) copy-start(f32[6]{0:T(128)} %param.22) | copy-start | bytes 76
Sparse Core Ops, SparseCore 0:
  9.5 115.6 all-gather.2
